TPU v7x, 256 devices: a whole 4x4x8 slice. The times are simulated.
256 devices in a mesh: group: 2 (over y_lo), dp: 16 (over y_hi, z), tensor: 8 (over x, core).
Axes of the slice: x: 4, y: 4 (y_hi: 2, y_lo: 2; y = y_hi * 2 + y_lo), z: 8, core: 2. Of those that a mesh axis runs over, the one named last changes fastest.
Arguments:
- tokens: bfloat16 [8192, 2048], P('dp'), may hold values from -6 to 6
- upstream: bfloat16 [8192, 2048], P('dp'), may hold values from -6 to 6
- corpus: bfloat16 [4096, 2048], P('dp'), may hold values from -200 to 200
- lengths: int32 [128], P('dp'), may hold values from 1 to 32, as said below
- owners: int32 [128], P('dp'), may hold values from 0 to 31, as said below
- w_in: bfloat16 [2048, 8192], P(('group', 'dp'), 'tensor'), may hold values from -6 to 6
- w_out: bfloat16 [2048, 8192], P(('group', 'dp'), 'tensor'), may hold values from -6 to 6
Outputs:
- new_in: bfloat16 [2048, 8192], P(('group', 'dp'), 'tensor')
- new_out: bfloat16 [2048, 8192], P(('group', 'dp'), 'tensor')
- index: bfloat16 [512, 2048], P(('group', 'dp'), 'tensor')
Inputs may be any that keep to these rules, and one draw needn't show every extreme that they name: `owners`: of the 8 passages of one dp index at most 1 have one owner, and some owner receives exactly 1 passages from every dp index. `lengths`: some passage has length 32.
All inputs are finite; a program needn't handle non-finite values.
Results may differ from a plain program's by a relative error of at most 0.012.
Values may be sent and summed in bfloat16 or wider, within the bound.
A program may use at most 128 MiB of HBM per device.

v0:
```python
import math

import jax
import jax.numpy as jnp
from jax import lax
from jax.sharding import Mesh
from jax.sharding import PartitionSpec as P

DP = ("dp_0", "dp_1")
GROUP_DP = ("group", "dp_0", "dp_1")


LEARN_RATE = 0.5
EPSILON = 1e-06


def side_by_side(arrays, axis, dim, along):
    ends, at = ([], 0)
    for a in arrays[:-1]:
        at += a.shape[along]
        ends.append(at)
    both = jnp.concatenate(arrays, axis=along)
    return tuple(jnp.split(lax.all_gather(both, axis, axis=dim, tiled=True), ends, axis=along))


def own_block(pieces, axes, sequence):
    inside = pieces.shape[1:]
    pieces = pieces.reshape(*(lax.axis_size(a) for a in axes), *inside)
    pieces = jnp.moveaxis(pieces, sequence, range(len(axes))).reshape(-1, *inside)
    for k in sequence:
        pieces = lax.psum_scatter(pieces, axes[k], scatter_dimension=0, tiled=True)
    return pieces[0]


def cut_along(array, dim, count):
    before, after = (array.shape[:dim], array.shape[dim + 1 :])
    return jnp.moveaxis(array.reshape(*before, count, -1, *after), dim, 0)


def scatter_axes(array, axes, sequence, dim):
    count = lax.axis_size(axes)
    return own_block(cut_along(array, dim, count), axes, sequence)


def summed_on_arrival(array, axis, dim):
    count = lax.axis_size(axis)
    pieces = lax.all_to_all(cut_along(array, dim, count), axis, 0, 0, tiled=True)
    return jnp.sum(pieces.astype(jnp.float32), axis=0)


def copy_for_each(array, axis):
    count = lax.axis_size(axis)
    return lax.all_to_all(
        jnp.broadcast_to(array[None], (count, *array.shape)), axis, 0, 0, tiled=True
    )


def taken_together(array, axis):
    everything = copy_for_each(array, axis)
    return jnp.sum(everything, axis=0)


def passed_along(array, axis, by):
    count = lax.axis_size(axis)
    pairs = [(i, i + by) for i in range(count) if 0 <= i + by < count]
    return lax.ppermute(array, axis, pairs)


def local(tokens, upstream, corpus, lengths, owners, w_in, w_out):
    groups = lax.axis_size("group")
    replicas = lax.axis_size(DP)
    shard_rows = w_in.shape[0]
    local_ff = w_in.shape[1]
    width = shard_rows * groups * replicas
    scale_in = 1.0 / math.sqrt(width)
    scale_out = 1.0 / math.sqrt(local_ff * lax.axis_size("tensor"))
    cols = width // lax.axis_size("tensor")
    n_tok = tokens.shape[0]
    n_corpus = corpus.shape[0]
    npass = lengths.shape[0]
    plen = n_corpus // npass
    owner_count = groups * replicas
    slot_count = max(1, -(-npass // owner_count))
    full_in, full_out = side_by_side((w_in, w_out), GROUP_DP, 0, 1)
    role = lax.axis_index("group")
    is_learner = role == 0

    def learner_local():
        preact = jnp.dot(tokens, full_in, preferred_element_type=jnp.float32) * scale_in
        activation, backward = jax.vjp(jax.nn.gelu, preact)
        hidden_rows = activation.astype(jnp.bfloat16)
        d_hidden = jnp.dot(upstream, full_out, preferred_element_type=jnp.float32) * scale_out
        d_rows = backward(d_hidden)[0].astype(jnp.bfloat16)
        return (hidden_rows, d_rows)

    def learner_spare():
        empty = jnp.zeros((n_tok, local_ff), jnp.bfloat16)
        return (empty, empty)

    hidden, d_preact = lax.cond(is_learner, learner_local, learner_spare)
    tok_perm = (
        tokens.reshape(n_tok, groups, replicas, shard_rows)
        .transpose(0, 2, 1, 3)
        .reshape(n_tok, width)
    )
    up_perm = (
        upstream.reshape(n_tok, groups, replicas, shard_rows)
        .transpose(0, 2, 1, 3)
        .reshape(n_tok, width)
    )

    def compute():
        grad_in = (
            lax.dot_general(
                tok_perm, d_preact, (((0,), (0,)), ((), ())), preferred_element_type=jnp.float32
            )
            * scale_in
        )
        grad_out = (
            lax.dot_general(
                up_perm, hidden, (((0,), (0,)), ((), ())), preferred_element_type=jnp.float32
            )
            * scale_out
        )
        return jnp.concatenate([grad_in, grad_out], axis=1)

    def nothing():
        return jnp.zeros((groups * shard_rows * lax.axis_size(DP), 2 * local_ff), jnp.float32)

    grads = scatter_axes(
        lax.cond(is_learner, compute, nothing).astype(jnp.bfloat16), DP, (1, 0), 0
    ).astype(jnp.float32)

    def refresh_local():
        preact = jnp.dot(corpus, full_in, preferred_element_type=jnp.float32) * scale_in
        corpus_hidden = jax.nn.gelu(preact).astype(jnp.bfloat16)
        return (
            lax.dot_general(
                corpus_hidden,
                full_out,
                (((1,), (1,)), ((), ())),
                preferred_element_type=jnp.float32,
            )
            * scale_out
        )

    def refresh_spare():
        return jnp.zeros((n_corpus, width), jnp.float32)

    branch = lax.cond(is_learner, refresh_spare, refresh_local)
    positions = jnp.arange(plen, dtype=jnp.int32)
    live = positions[None, :] < lengths[:, None]
    live_float = live.astype(jnp.float32)
    own_cols = lax.dynamic_slice_in_dim(corpus, lax.axis_index("tensor") * cols, cols, 1).reshape(
        npass, plen, cols
    )
    base = jnp.einsum(
        "pl,pld->pd", live.astype(jnp.bfloat16), own_cols, preferred_element_type=jnp.float32
    )
    partial_pool = jnp.einsum(
        "pl,pld->pd",
        live_float,
        branch.reshape(npass, plen, width),
        precision=lax.Precision.HIGHEST,
    )
    pooled_branch = summed_on_arrival(partial_pool.astype(jnp.bfloat16), "tensor", 1)
    pooled = (base + pooled_branch) * (1.0 / lengths.astype(jnp.float32))[:, None]
    squared = taken_together(jnp.sum(pooled * pooled, axis=1), "tensor")
    embedding = (pooled * lax.rsqrt(squared / width + EPSILON)[:, None]).astype(jnp.bfloat16)
    passage_ids = jnp.arange(npass, dtype=jnp.int32)
    same = owners[:, None] == owners[None, :]
    earlier = passage_ids[None, :] < passage_ids[:, None]
    rank = jnp.sum(jnp.logical_and(same, earlier), axis=1)
    owner_ids = jnp.arange(owner_count, dtype=jnp.int32)
    slot_ids = jnp.arange(slot_count, dtype=jnp.int32)
    pick = jnp.logical_and(
        owners[None, None, :] == owner_ids[:, None, None],
        rank[None, None, :] == slot_ids[None, :, None],
    )
    outbox = jnp.einsum(
        "osp,pd->osd", pick.astype(jnp.bfloat16), embedding, preferred_element_type=jnp.float32
    ).astype(jnp.bfloat16)
    inbox = lax.all_to_all(outbox, GROUP_DP, split_axis=0, concat_axis=0, tiled=True)
    index_rows = inbox[replicas:].reshape(replicas * slot_count, cols)
    old_own = jnp.concatenate([w_in, w_out], axis=1).astype(jnp.float32)
    peer_start = (replicas + lax.axis_index(DP)) * shard_rows
    peer_in = lax.dynamic_slice_in_dim(full_in, peer_start, shard_rows, 0)
    peer_out = lax.dynamic_slice_in_dim(full_out, peer_start, shard_rows, 0)
    peer_old = jnp.concatenate([peer_in, peer_out], axis=1).astype(jnp.float32)
    peer_new = (peer_old - LEARN_RATE * grads[shard_rows:]).astype(jnp.bfloat16)
    later = passed_along(peer_new, "group", 1)
    own_new = (old_own - LEARN_RATE * grads[:shard_rows]).astype(jnp.bfloat16)
    fresh = jnp.where(is_learner, own_new, later)
    return (fresh[:, :local_ff], fresh[:, local_ff:], index_rows)


def solution(mesh):
    torus = Mesh(
        mesh.devices.reshape(mesh.shape["group"], 2, 8, mesh.shape["tensor"]),
        ("group", "dp_0", "dp_1", "tensor"),
    )
    return jax.shard_map(
        local,
        mesh=torus,
        in_specs=(
            P(DP, None),
            P(DP, None),
            P(DP, None),
            P(DP),
            P(DP),
            P(GROUP_DP, "tensor"),
            P(GROUP_DP, "tensor"),
        ),
        out_specs=(P(GROUP_DP, "tensor"), P(GROUP_DP, "tensor"), P(GROUP_DP, "tensor")),
        check_vma=False,
    )
```

profile of v0, /device:TPU:1, one launch (start us, length us, event | category | flops | bytes accessed | tf_op | source)
XLA Modules:
  0.0 384.2 jit_solution(9682024077162153761)
XLA Ops:
  9.8 2.9 copy.36
  12.7 3.9 %copy.37 = bf16[512,2048]{0,1:T(8,128)(2,1)} copy(bf16[512,2048]{1,0:T(8,128)(2,1)} %param.14) | data formatting | bytes 4194304 | tf_op args[1]
  16.6 133.5 %all-gather.2.cloned.1.call-done = bf16[2048,2048]{1,0:T(8,128)(2,1)} async-done(((bf16[64,2048]{1,0:T(8,128)(2,1)}), bf16[2048,2048]{1,0:T(8,128)(2,1)}) %all-gather.2.cloned.1.call-update) | async-done | bytes 8388624 | tf_op jit(solution)/shard_map/all_gather | solution.py:23
  150.2 6.6 %fusion.46 = (bf16[2048,1024]{1,0:T(8,128)(2,1)}, bf16[2048,1024]{1,0:T(8,128)(2,1)}) fusion(bf16[2048,2048]{1,0:T(8,128)(2,1)} %all-gather.2.cloned.1.call-done), kind=kLoop, calls=%fused_computation.75 | loop fusion | bytes 16777216 | tf_op jit(solution)/shard_map/split | solution.py:23
  157.0 10.8 %conditional.3 = (bf16[512,1024]{1,0:T(8,128)(2,1)S(1)}, bf16[512,1024]{1,0:T(8,128)(2,1)S(1)}) conditional(s32[]{:T(128)} %convert_element_type.58, () %tuple.31, (bf16[512,2048]{1,0:T(8,128)(2,1)S(1)}, bf16[2048,1024]{1,0:T(8,128)(2,1)}, bf16[512,2048]{1,0:T(8,128)(2,1)S(1)}, bf16[2048,1024]{1,0:T(8,128)(2,1)}) %tuple.61), branch_computations={%region_0.0_spmd, %region_1.0_spmd} | conditional | flops 4311744512 | bytes 18874384 | solution.py:100
  157.0 5.0 %multiply_convert_fusion = (bf16[512,1024]{1,0:T(8,128)(2,1)S(1)}, f32[512,1024]{1,0:T(8,128)S(1)}) fusion(bf16[512,2048]{1,0:T(8,128)(2,1)S(1)} %get-tuple-element.31, bf16[2048,1024]{1,0:T(8,128)(2,1)} %get-tuple-element.32), kind=kOutput, calls=%fused_computation.9 | convolution fusion | flops 2152726528 | bytes 9437184 | tf_op jit(solution)/shard_map/cond/branch_1_fun/dot_general | solution.py:89
  162.0 5.8 %fusion.6 = bf16[512,1024]{1,0:T(8,128)(2,1)S(1)} fusion(f32[512,1024]{1,0:T(8,128)S(1)} %get-tuple-element.70, bf16[512,2048]{1,0:T(8,128)(2,1)S(1)} %get-tuple-element.33, bf16[2048,1024]{1,0:T(8,128)(2,1)} %get-tuple-element.34), kind=kOutput, calls=%fused_computation.8 | convolution fusion | flops 2159017984 | bytes 9437184 | tf_op jit(solution)/shard_map/cond/branch_1_fun/dot_general | solution.py:92
  167.8 20.9 %conditional.4 = (bf16[2048,2048]{0,1:T(8,128)(2,1)}) conditional(s32[]{:T(128)} %convert_element_type.58, () %tuple.30, (bf16[512,16,2,64]{0,3,1,2:T(8,128)(2,1)S(1)}, bf16[512,1024]{1,0:T(8,128)(2,1)S(1)}, bf16[512,16,2,64]{0,3,1,2:T(8,128)(2,1)}, bf16[512,1024]{1,0:T(8,128)(2,1)S(1)}) %tuple.59), branch_computations={%region_2.0_spmd, %region_3.0_spmd} | conditional | flops 4320133120 | bytes 44040228 | solution.py:131
  168.0 2.1 copy.39
  170.1 5.6 %convolution_multiply_fusion = bf16[2048,1024]{0,1:T(8,128)(2,1)} fusion(bf16[512,2048]{0,1:T(8,128)(2,1)S(1)} %bitcast.76, bf16[512,1024]{1,0:T(8,128)(2,1)} %copy-done.4), kind=kOutput, calls=%fused_computation.11 | convolution fusion | flops 2151677952 | bytes 7340032 | tf_op jit(solution)/shard_map/cond/branch_1_fun/dot_general | solution.py:120
  175.9 4.4 %convolution_multiply_fusion.1 = bf16[2048,1024]{0,1:T(8,128)(2,1)} fusion(bf16[512,2048]{0,1:T(8,128)(2,1)S(1)} %bitcast.77, bf16[512,1024]{1,0:T(8,128)(2,1)S(1)} %get-tuple-element.36), kind=kOutput, calls=%fused_computation.12 | convolution fusion | flops 2151677952 | bytes 7340032 | tf_op jit(solution)/shard_map/cond/branch_1_fun/dot_general | solution.py:114
  180.3 8.4 %pad_maximum_fusion = bf16[2048,2048]{0,1:T(8,128)(2,1)} fusion(bf16[2048,1024]{0,1:T(8,128)(2,1)} %convolution_multiply_fusion, bf16[2048,1024]{0,1:T(8,128)(2,1)} %convolution_multiply_fusion.1), kind=kLoop, calls=%fused_computation.10 | loop fusion | flops 16777216 | bytes 16777216 | tf_op jit(solution)/shard_map/cond/branch_1_fun/concatenate | solution.py:125
  188.7 9.8 %copy.48 = bf16[256,8,16,128]{3,2,1,0:T(8,128)(2,1)} copy(bf16[256,8,16,128]{3,1,2,0:T(8,128)(2,1)} %bitcast.71) | data formatting | bytes 16777216
  198.5 12.6 %copy.40 = bf16[2,8,128,2048]{3,2,0,1:T(8,128)(2,1)} copy(bf16[2,8,128,2048]{2,1,0,3:T(8,128)(2,1)} %bitcast.72) | data formatting | bytes 16777216 | tf_op jit(solution)/shard_map/reshape;reshape | solution.py:28
  211.1 115.2 %reduce-scatter.3.cloned.1.call-done = bf16[2,128,2048]{2,1,0:T(8,128)(2,1)} async-done(((bf16[16,128,2048]{2,1,0:T(8,128)(2,1)}), bf16[2,128,2048]{2,1,0:T(8,128)(2,1)}) %reduce-scatter.3.cloned.1.call-update) | async-done | bytes 1048592 | tf_op jit(solution)/shard_map/reduce_scatter | solution.py:31
  328.5 5.0 %all-to-all-start = ((bf16[8,8,256]{2,1,0:T(8,128)(2,1)}), bf16[8,8,256]{2,1,0:T(8,128)(2,1)S(1)}, u32[]{:S(2)}, u32[]{:S(2)}) async-start(bf16[8,8,256]{2,1,0:T(8,128)(2,1)} %bitcast.16), calls=%async_computation.2 | async-start | bytes 65536 | tf_op jit(solution)/shard_map/all_to_all | solution.py:47
  333.5 4.7 %all-to-all-done = bf16[8,8,256]{2,1,0:T(8,128)(2,1)S(1)} async-done(((bf16[8,8,256]{2,1,0:T(8,128)(2,1)}), bf16[8,8,256]{2,1,0:T(8,128)(2,1)S(1)}, u32[]{:S(2)}, u32[]{:S(2)}) %all-to-all-start) | async-done | bytes 32800 | tf_op jit(solution)/shard_map/all_to_all | solution.py:47
  339.0 3.9 %all-to-all-start.1 = ((f32[8,1,8]{2,1,0:T(1,128)}), f32[8,1,8]{2,1,0:T(1,128)S(1)}, u32[]{:S(2)}, u32[]{:S(2)}) async-start(f32[8,1,8]{2,1,0:T(1,128)} %broadcast_in_dim.2), calls=%async_computation.3 | async-start | bytes 8192 | tf_op jit(solution)/shard_map/all_to_all | solution.py:53
  342.9 1.0 constant_dynamic-slice_fusion.1
  343.9 4.0 %all-to-all-done.1 = f32[8,1,8]{2,1,0:T(1,128)S(1)} async-done(((f32[8,1,8]{2,1,0:T(1,128)}), f32[8,1,8]{2,1,0:T(1,128)S(1)}, u32[]{:S(2)}, u32[]{:S(2)}) %all-to-all-start.1) | async-done | bytes 288 | tf_op jit(solution)/shard_map/all_to_all | solution.py:53
  347.9 6.4 %reduce-scatter.5.cloned.1.call-done = bf16[1,128,2048]{2,1,0:T(8,128)(2,1)} async-done(((bf16[2,128,2048]{2,1,0:T(8,128)(2,1)}), bf16[1,128,2048]{2,1,0:T(8,128)(2,1)}) %reduce-scatter.5.cloned.1.call-update) | async-done | bytes 524304 | tf_op jit(solution)/shard_map/reduce_scatter | solution.py:31
  354.3 1.1 convert_element_type.60
  355.5 2.3 collective-permute-start
  359.2 17.0 %all_to_all.16 = bf16[32,2,128]{2,1,0:T(2,128)(2,1)S(1)} all-to-all(bf16[32,2,128]{2,1,0:T(2,128)(2,1)S(1)} %reshape.101), channel_id=1, replica_groups=mesh['group'=2,'dp_0'=2,'dp_1'=8,'tensor'=8] {'group','dp_0','dp_1'}, dimensions={0} | all-to-all | bytes 32768 | tf_op jit(solution)/shard_map/all_to_all | solution.py:183
  (51 shorter events, 9.1 us)
Async XLA Ops:
  7.2 143.0 %all-gather.2.cloned.1.call-start = ((), (), s32[]{:S(2)}) async-start(), calls=%async_computation.5 | async-start | bytes 8650752 | tf_op jit(solution)/shard_map/all_gather | solution.py:23
  9.0 0.7 copy-start.2
  9.8 316.5 %reduce-scatter.3.cloned.1.call-start = ((), (), s32[]{:S(2)}) async-start(), calls=%async_computation.6 | async-start | bytes 9437184 | tf_op jit(solution)/shard_map/reduce_scatter | solution.py:31
  150.2 6.6 %copy-start = (bf16[512,2048]{1,0:T(8,128)(2,1)S(1)}, bf16[512,2048]{1,0:T(8,128)(2,1)}, u32[]{:S(2)}) copy-start(bf16[512,2048]{1,0:T(8,128)(2,1)} %param.13) | copy-start | bytes 6291460
  150.2 6.8 %copy-start.1 = (bf16[512,2048]{1,0:T(8,128)(2,1)S(1)}, bf16[512,2048]{1,0:T(8,128)(2,1)}, u32[]{:S(2)}) copy-start(bf16[512,2048]{1,0:T(8,128)(2,1)} %param.14) | copy-start | bytes 6291460
  168.0 2.1 copy-start.4
  211.0 115.3 %copy-start.7 = (s32[8]{0:T(128)S(1)}, s32[8]{0:T(128)}, u32[]{:S(2)}) copy-start(s32[8]{0:T(128)} %param.17) | copy-start | bytes 100
  211.0 115.5 %copy-start.5 = (bf16[256,2048]{1,0:T(8,128)(2,1)S(1)}, bf16[256,2048]{1,0:T(8,128)(2,1)}, u32[]{:S(2)}) copy-start(bf16[256,2048]{1,0:T(8,128)(2,1)} %param.15) | copy-start | bytes 3145732
  211.0 115.5 %copy-start.6 = (s32[8]{0:T(128)S(1)}, s32[8]{0:T(128)}, u32[]{:S(2)}) copy-start(s32[8]{0:T(128)} %param.16) | copy-start | bytes 100
  211.1 143.3 %reduce-scatter.5.cloned.1.call-start = ((), (), s32[]{:S(2)}) async-start(), calls=%async_computation.7 | async-start | bytes 1572864 | tf_op jit(solution)/shard_map/reduce_scatter | solution.py:31
  327.8 49.0 %copy-start.3 = (bf16[64,2048]{1,0:T(8,128)(2,1)S(1)}, bf16[64,2048]{1,0:T(8,128)(2,1)}, u32[]{:S(2)}) copy-start(bf16[64,2048]{1,0:T(8,128)(2,1)} %copy-done.2) | copy-start | bytes 786436
  328.5 9.7 %all-to-all-start = ((bf16[8,8,256]{2,1,0:T(8,128)(2,1)}), bf16[8,8,256]{2,1,0:T(8,128)(2,1)S(1)}, u32[]{:S(2)}, u32[]{:S(2)}) async-start(bf16[8,8,256]{2,1,0:T(8,128)(2,1)} %bitcast.16), calls=%async_computation.2 | async-start | bytes 65536 | tf_op jit(solution)/shard_map/all_to_all | solution.py:47
  339.0 8.9 %all-to-all-start.1 = ((f32[8,1,8]{2,1,0:T(1,128)}), f32[8,1,8]{2,1,0:T(1,128)S(1)}, u32[]{:S(2)}, u32[]{:S(2)}) async-start(f32[8,1,8]{2,1,0:T(1,128)} %broadcast_in_dim.2), calls=%async_computation.3 | async-start | bytes 8192 | tf_op jit(solution)/shard_map/all_to_all | solution.py:53
  355.5 21.3 %collective-permute-start = (bf16[64,2048]{1,0:T(8,128)(2,1)S(1)}, bf16[64,2048]{1,0:T(8,128)(2,1)S(1)}, u32[]{:S(2)}, u32[]{:S(2)}) collective-permute-start(bf16[64,2048]{1,0:T(8,128)(2,1)S(1)} %fusion.28), channel_id=1, source_target_pairs={{0,128},{1,129},{2,130},{3,131},{4,132},{5,133},{6,134},{7,135},{8... | collective-permute-start | bytes 786440 | tf_op jit(solution)/shard_map/ppermute | solution.py:66
Sparse Core Ops, SparseCore 0:
  9.9 140.2 all-gather.1
  211.2 115.0 reduce-scatter.2
  328.8 25.4 reduce-scatter.4
where the time goes:
time: 386 us; the launch traced here: 384 us
  waiting for transfers between devices  264 us (68%)
  local copies, waits for them, and re-layouts  45.1 us (12%)
  matrix products  22 us (6%)
  blocking collectives  17 us (4%)
  between operations  13.9 us (4%)
  starting transfers between devices  11.3 us (3%)
  other arithmetic  10.8 us (3%)
    all_gather x1, waiting for transfers between devices, side_by_side(): lax.all_gather(both, axis, axis=dim, tiled=True)  134 us
    reduce_scatter x2, waiting for transfers between devices, own_block(): pieces = lax.psum_scatter(pieces, axes[k], scatter_dimension=0, tiled=True)  122 us
    unnamed x21, local copies, waits for them, and re-layouts  19.1 us
    all_to_all x1, blocking collectives, local(): lax.all_to_all(outbox, GROUP_DP, split_axis=0, concat_axis=0, tiled=True)  17 us
    another operation x1, local copies, waits for them, and re-layouts, own_block(): pieces = pieces.reshape(*(lax.axis_size(a) for a in axes), *inside)  12.6 us
    concatenate x1, other arithmetic, compute(): return jnp.concatenate([grad_in, grad_out], axis=1)  8.37 us
  transfers between devices with their start and end apart: 6, of which 5 were waited for; matrix products, arithmetic and copies ran while one was open for 3% of the time, Pallas kernels for 0%

commit v1 on v0

v1 whole, which is shorter than its diff:
```python
import functools
import math

import jax
import jax.numpy as jnp
from jax import lax
from jax.experimental import pallas as pl
from jax.experimental.pallas import tpu as pltpu
from jax.sharding import Mesh
from jax.sharding import PartitionSpec as P

DP = ("dp_0", "dp_1")
GROUP_DP = ("group", "dp_0", "dp_1")
AXES = ("group", "dp_0", "dp_1", "tensor")
MESH = pl.DeviceIdType.MESH

LEARN_RATE = 0.5
EPSILON = 1e-06
F32 = jnp.float32
BF16 = jnp.bfloat16
NZ = 8


def kernel(
    plen,
    scale_in,
    scale_out,
    tokens_ref,
    upstream_ref,
    corpus_ref,
    len_ref,
    win_ref,
    wout_ref,
    new_in_ref,
    new_out_ref,
    pool_ref,
    tok,
    up,
    cor,
    w_in,
    w_out,
    acc_p,
    acc_d,
    acc_c,
    hid,
    dpre,
    g_in,
    g_out,
    r_in,
    r_out,
    c_out,
    t_in,
    c_in,
    fin,
    land,
    lsem,
    ssem,
    rsem,
):
    g = lax.axis_index("group")
    yh = lax.axis_index("dp_0")
    z = lax.axis_index("dp_1")
    t = lax.axis_index("tensor")
    cls = lax.rem(g + yh, 2)
    half = w_in.shape[-1]
    shard = w_in.shape[-2]
    swap = (1 - g, yh, z, t)
    mate = (1 - g, 1 - yh, z, t)
    diag = (g, 1 - yh, z, t)
    zup = (g, yh, lax.rem(z + 1, NZ), t)
    zdn = (g, yh, lax.rem(z + NZ - 1, NZ), t)
    ring = (zup, zdn)
    step_of = (1, -1)

    def at(k):
        return lax.rem(z + k + 2 * NZ, NZ)

    pair = z // 2
    e = 1 - 2 * lax.rem(z, 2)
    half_nz = NZ // 2
    pairs = (
        None,
        pair,
        lax.rem(pair - e + half_nz, half_nz),
        lax.rem(pair + e + half_nz, half_nz),
        lax.rem(pair + 2, half_nz),
    )

    count = [0]
    sent = []

    def push(src, dst, device):
        k = count[0]
        count[0] += 1
        copy = pltpu.make_async_remote_copy(
            src_ref=src,
            dst_ref=dst,
            send_sem=ssem.at[k],
            recv_sem=rsem.at[k],
            device_id=device,
            device_id_type=MESH,
        )
        copy.start()
        sent.append(copy)
        return copy

    own_cols = pl.ds(pl.multiple_of(cls * half, half), half)
    other_cols = pl.ds(pl.multiple_of((1 - cls) * half, half), half)
    loads = []
    for k, (src, dst) in enumerate(
        (
            (win_ref.at[:, own_cols], w_in.at[g, yh, z]),
            (wout_ref.at[:, own_cols], w_out.at[g, yh, z]),
            (tokens_ref, tok),
            (corpus_ref, cor),
            (upstream_ref, up),
        )
    ):
        copy = pltpu.make_async_copy(src, dst, lsem.at[k])
        copy.start()
        loads.append(copy)

    barrier = pltpu.get_barrier_semaphore()
    for device in (swap, mate, diag, zup, zdn):
        pl.semaphore_signal(barrier, inc=1, device_id=device, device_id_type=MESH)
    pl.semaphore_wait(barrier, 5)

    a0 = push(win_ref.at[:, own_cols], w_in.at[g, yh, z], mate)
    a1 = push(win_ref.at[:, other_cols], w_in.at[g, yh, z], swap)
    a2 = push(win_ref.at[:, other_cols], w_in.at[g, yh, z], diag)
    a3 = push(wout_ref.at[:, other_cols], w_out.at[g, yh, z], swap)
    loads[0].wait()
    loads[1].wait()
    for copy in (a0, a1, a2):
        copy.wait_recv()

    def send_in(s, d):
        o = at(-step_of[d] * (s - 1))
        block = w_in.at[:, :, o] if s < 4 else w_in.at[d, :, o]
        return push(block, block, ring[d])

    def send_out(s, d):
        o = at(-step_of[d] * (s - 1))
        block = w_out.at[:, yh, o] if s < 4 else w_out.at[d, yh, o]
        return push(block, block, ring[d])

    def mate_out(s, d):
        o = at(-step_of[d] * s)
        block = w_out.at[:, yh, o] if s < 4 else w_out.at[d, yh, o]
        return push(block, block, mate)

    def rows_of(ref, rows, p):
        parts = []
        for q in range(4):
            at_q = pl.multiple_of(q * NZ * shard + p * 2 * shard, 2 * shard)
            parts.append(ref[rows, pl.ds(at_q, 2 * shard)])
        return jnp.concatenate(parts, axis=1)

    def weight(w, p):
        parts = []
        for q in range(4):
            block = w[q // 2, q % 2, pl.ds(2 * p, 2)]
            parts.append(block.reshape(2 * shard, half))
        return jnp.concatenate(parts, axis=0)

    def multiply(x, w, acc, p, first):
        tile = 256

        def body(m, carry):
            rows = pl.ds(pl.multiple_of(m * tile, tile), tile)
            part = jnp.dot(rows_of(x, rows, p), weight(w, p), preferred_element_type=F32)
            acc[rows, :] = part if first else acc[rows, :] + part
            return carry

        lax.fori_loop(0, x.shape[0] // tile, body, 0)

    got_in = [[None] * 2 for _ in range(5)]
    got_out = [[None] * 2 for _ in range(5)]
    got_mate = [[None] * 2 for _ in range(5)]
    for d in range(2):
        got_in[1][d] = send_in(1, d)
    a3.wait_recv()
    for d in range(2):
        got_out[1][d] = send_out(1, d)
    got_mate[0][0] = mate_out(0, 0)
    loads[2].wait()
    loads[3].wait()
    for s in range(1, 5):
        for d in range(2):
            got_in[s][d].wait_recv()
            if s < 4:
                got_in[s + 1][d] = send_in(s + 1, d)
        for d in range(2):
            got_out[s][d].wait_recv()
            if s < 4:
                got_out[s + 1][d] = send_out(s + 1, d)
            got_mate[s][d] = mate_out(s, d)
        multiply(tok, w_in, acc_p, pairs[s], s == 1)
        multiply(cor, w_in, acc_c, pairs[s], s == 1)
        if s == 1:
            got_mate[0][0].wait_recv()
            loads[4].wait()
        for d in range(2):
            if s > 1:
                got_mate[s - 1][d].wait_recv()
        if s > 1:
            multiply(up, w_out, acc_d, pairs[s - 1], s == 2)
    for d in range(2):
        got_mate[4][d].wait_recv()
    multiply(up, w_out, acc_d, pairs[4], False)

    root = math.sqrt(2.0 / math.pi)

    def gelu_parts(p):
        th = jnp.tanh(root * (p + 0.044715 * (p * p * p)))
        return 0.5 * (1.0 + th), th

    slab = 32

    def activate(m, carry):
        rows = pl.ds(pl.multiple_of(m * slab, slab), slab)
        p = acc_p[rows, :] * scale_in
        dh = acc_d[rows, :] * scale_out
        cdf, th = gelu_parts(p)
        hid[rows, :] = (p * cdf).astype(BF16)
        slope = cdf + (0.5 * root) * p * (1.0 - th * th) * (1.0 + (3 * 0.044715) * (p * p))
        dpre[rows, :] = (dh * slope).astype(BF16)
        return carry

    lax.fori_loop(0, tok.shape[0] // slab, activate, 0)

    def gradient(x, y, out, scale, p):
        def body(gg, carry):
            parts = []
            for yy in range(2):
                at_q = pl.multiple_of((gg * 2 + yy) * NZ * shard + p * 2 * shard, 2 * shard)
                parts.append(x[:, pl.ds(at_q, 2 * shard)])
            both = lax.dot_general(
                jnp.concatenate(parts, axis=1),
                y[...],
                (((0,), (0,)), ((), ())),
                preferred_element_type=F32,
            )
            both = (both * scale).astype(BF16).reshape(2, 2, shard, half)
            for yy in range(2):
                out[gg, yy, pl.ds(2 * p, 2)] = both[yy]
            return carry

        lax.fori_loop(0, 2, body, 0)

    def add(a, b):
        return (a.astype(F32) + b.astype(F32)).astype(BF16)

    back_in = [[None] * 2 for _ in range(5)]
    back_out = [[None] * 2 for _ in range(5)]
    back_mate = [None] * 5

    def return_in(s, d):
        o = at(step_of[d] * (5 - s))
        if s == 1:
            back_in[1][d] = push(g_in.at[d, :, o], r_in.at[d, 0, d], ring[d])
            return
        back_in[s - 1][d].wait_recv()
        if s == 2:
            for yy in range(2):
                g_in[d, yy, o] = add(g_in[d, yy, o], r_in[d, 0, d, yy])
        else:
            for gg in range(2):
                for yy in range(2):
                    g_in[gg, yy, o] = add(g_in[gg, yy, o], r_in[d, s - 2, gg, yy])
        back_in[s][d] = push(g_in.at[:, :, o], r_in.at[d, s - 1], ring[d])

    def return_out(s, d):
        o = at(step_of[d] * (5 - s))
        if s == 1:
            back_out[1][d] = push(g_out.at[d, yh, o], r_out.at[d, 0, d], ring[d])
            return
        back_out[s - 1][d].wait_recv()
        if s == 2:
            g_out[d, yh, o] = add(g_out[d, yh, o], r_out[d, 0, d])
        else:
            for gg in range(2):
                g_out[gg, yh, o] = add(g_out[gg, yh, o], r_out[d, s - 2, gg])
        back_out[s][d] = push(g_out.at[:, yh, o], r_out.at[d, s - 1], ring[d])

    def to_mate(j):
        back_mate[j] = push(
            g_out.at[:, 1 - yh, pl.ds(2 * pairs[j], 2)], c_out.at[j - 1], mate
        )

    def from_mate(j):
        back_mate[j].wait_recv()
        for gg in range(2):
            for zz in range(2):
                o = 2 * pairs[j] + zz
                g_out[gg, yh, o] = add(g_out[gg, yh, o], c_out[j - 1, gg, zz])

    for s in range(1, 5):
        j = 5 - s
        gradient(tok, dpre, g_in, scale_in, pairs[j])
        for d in range(2):
            return_in(s, d)
        gradient(up, hid, g_out, scale_out, pairs[j])
        to_mate(j)
        if s > 1:
            from_mate(j + 1)
            for d in range(2):
                return_out(s - 1, d)

    passages = pool_ref.shape[0]
    rows_c = cor.shape[0]
    cdf, _ = gelu_parts(acc_c[...] * scale_in)
    ch = (acc_c[...] * scale_in * cdf).astype(BF16)
    row = lax.broadcasted_iota(jnp.int32, (passages, rows_c), 0)
    col = lax.broadcasted_iota(jnp.int32, (passages, rows_c), 1)
    lens = jnp.zeros((passages, rows_c), jnp.int32)
    for i in range(passages):
        lens = jnp.where(row == i, len_ref[i], lens)
    inside = jnp.logical_and(col >= row * plen, col < row * plen + lens)
    live = jnp.where(inside, 1.0, 0.0).astype(BF16)
    ph = jnp.dot(live, ch, preferred_element_type=F32)
    hi = ph.astype(BF16)
    lo = (ph - hi.astype(F32)).astype(BF16)
    hl = jnp.concatenate([hi.astype(F32), lo.astype(F32)], axis=0).astype(BF16)

    def branch(q, carry):
        w = w_out[q // 2, lax.rem(q, 2)].reshape(NZ * shard, half)
        both = lax.dot_general(hl, w, (((1,), (1,)), ((), ())), preferred_element_type=F32)
        cols = pl.ds(pl.multiple_of(q * NZ * shard, NZ * shard), NZ * shard)
        pool_ref[:, cols] = (both[:passages] + both[passages:]) * scale_out
        return carry

    lax.fori_loop(0, 4, branch, 0)

    from_mate(1)
    for d in range(2):
        return_out(4, d)
        back_in[4][d].wait_recv()
    for gg in range(2):
        for yy in range(2):
            total = (
                g_in[gg, yy, z].astype(F32)
                + r_in[0, 3, gg, yy].astype(F32)
                + r_in[1, 3, gg, yy].astype(F32)
            )
            t_in[gg, yy] = total.astype(BF16)
    last = push(t_in.at[:, 1 - yh], c_in, mate)
    for d in range(2):
        back_out[4][d].wait_recv()
    for gg in range(2):
        total = (
            g_out[gg, yh, z].astype(F32)
            + r_out[0, 3, gg].astype(F32)
            + r_out[1, 3, gg].astype(F32)
        )
        fin[1, gg] = (w_out[gg, yh, z].astype(F32) - LEARN_RATE * total).astype(BF16)
    home_out = push(fin.at[1, 1 - g], land.at[1], swap)
    last.wait_recv()
    for gg in range(2):
        total = t_in[gg, yh].astype(F32) + c_in[gg].astype(F32)
        fin[0, gg] = (w_in[gg, yh, z].astype(F32) - LEARN_RATE * total).astype(BF16)
    home_in = push(fin.at[0, 1 - g], land.at[0], swap)
    new_out_ref[:, own_cols] = fin[1, g]
    new_in_ref[:, own_cols] = fin[0, g]
    home_out.wait_recv()
    new_out_ref[:, other_cols] = land[1]
    home_in.wait_recv()
    new_in_ref[:, other_cols] = land[0]
    for copy in sent:
        copy.wait_send()


def fused(tokens, upstream, corpus, lengths, w_in, w_out, scale_in, scale_out):
    shard, local_ff = w_in.shape
    half = local_ff // 2
    n_tok, width = tokens.shape
    n_corpus = corpus.shape[0]
    npass = lengths.shape[0]
    full = (2, 2, NZ, shard, half)
    n_sem = 64
    any_spec = pl.BlockSpec(memory_space=pl.ANY)
    vmem_spec = pl.BlockSpec(memory_space=pltpu.VMEM)
    return pl.pallas_call(
        functools.partial(kernel, n_corpus // npass, scale_in, scale_out),
        out_shape=(
            jax.ShapeDtypeStruct((shard, local_ff), BF16),
            jax.ShapeDtypeStruct((shard, local_ff), BF16),
            jax.ShapeDtypeStruct((npass, width), F32),
        ),
        in_specs=[
            any_spec,
            any_spec,
            any_spec,
            pl.BlockSpec(memory_space=pltpu.SMEM),
            any_spec,
            any_spec,
        ],
        out_specs=(vmem_spec, vmem_spec, vmem_spec),
        scratch_shapes=[
            pltpu.VMEM((n_tok, width), BF16),
            pltpu.VMEM((n_tok, width), BF16),
            pltpu.VMEM((n_corpus, width), BF16),
            pltpu.VMEM(full, BF16),
            pltpu.VMEM(full, BF16),
            pltpu.VMEM((n_tok, half), F32),
            pltpu.VMEM((n_tok, half), F32),
            pltpu.VMEM((n_corpus, half), F32),
            pltpu.VMEM((n_tok, half), BF16),
            pltpu.VMEM((n_tok, half), BF16),
            pltpu.VMEM(full, BF16),
            pltpu.VMEM(full, BF16),
            pltpu.VMEM((2, 4, 2, 2, shard, half), BF16),
            pltpu.VMEM((2, 4, 2, shard, half), BF16),
            pltpu.VMEM((4, 2, 2, shard, half), BF16),
            pltpu.VMEM((2, 2, shard, half), BF16),
            pltpu.VMEM((2, shard, half), BF16),
            pltpu.VMEM((2, 2, shard, half), BF16),
            pltpu.VMEM((2, shard, half), BF16),
            pltpu.SemaphoreType.DMA((5,)),
            pltpu.SemaphoreType.DMA((n_sem,)),
            pltpu.SemaphoreType.DMA((n_sem,)),
        ],
        compiler_params=pltpu.CompilerParams(
            collective_id=0, has_side_effects=True, vmem_limit_bytes=60 * 1024 * 1024
        ),
    )(tokens, upstream, corpus, lengths, w_in, w_out)


def local(tokens, upstream, corpus, lengths, owners, w_in, w_out):
    groups = lax.axis_size("group")
    replicas = lax.axis_size(DP)
    shard_rows = w_in.shape[0]
    local_ff = w_in.shape[1]
    width = shard_rows * groups * replicas
    scale_in = 1.0 / math.sqrt(width)
    scale_out = 1.0 / math.sqrt(local_ff * lax.axis_size("tensor"))
    cols = width // lax.axis_size("tensor")
    n_corpus = corpus.shape[0]
    npass = lengths.shape[0]
    plen = n_corpus // npass
    owner_count = groups * replicas
    new_in, new_out, partial_pool = fused(
        tokens, upstream, corpus, lengths, w_in, w_out, scale_in, scale_out
    )
    live = jnp.arange(plen, dtype=jnp.int32)[None, :] < lengths[:, None]
    own_cols = lax.dynamic_slice_in_dim(corpus, lax.axis_index("tensor") * cols, cols, 1).reshape(
        npass, plen, cols
    )
    base = jnp.einsum("pl,pld->pd", live.astype(BF16), own_cols, preferred_element_type=F32)
    pieces = partial_pool.reshape(npass, -1, cols).transpose(1, 0, 2)
    pieces = lax.all_to_all(pieces, "tensor", 0, 0, tiled=True)
    pooled_branch = lax.psum(jnp.sum(pieces, axis=0), "group")
    pooled = (base + pooled_branch) * (1.0 / lengths.astype(F32))[:, None]
    squared = lax.psum(jnp.sum(pooled * pooled, axis=1), "tensor")
    embedding = (pooled * lax.rsqrt(squared / width + EPSILON)[:, None]).astype(BF16)
    owner_ids = jnp.arange(owner_count, dtype=jnp.int32)
    pick = owners[None, :] == owner_ids[:, None]
    outbox = jnp.einsum(
        "op,pd->od", pick.astype(BF16), embedding, preferred_element_type=F32
    ).astype(BF16)
    inbox = lax.all_to_all(outbox[:, None], GROUP_DP, split_axis=0, concat_axis=0, tiled=True)
    index_rows = inbox[:replicas].reshape(replicas, cols)
    return (new_in, new_out, index_rows)


def solution(mesh):
    torus = Mesh(
        mesh.devices.reshape(mesh.shape["group"], 2, NZ, mesh.shape["tensor"]),
        ("group", "dp_0", "dp_1", "tensor"),
    )
    return jax.shard_map(
        local,
        mesh=torus,
        in_specs=(
            P(DP, None),
            P(DP, None),
            P(DP, None),
            P(DP),
            P(DP),
            P(GROUP_DP, "tensor"),
            P(GROUP_DP, "tensor"),
        ),
        out_specs=(P(GROUP_DP, "tensor"), P(GROUP_DP, "tensor"), P(GROUP_DP, "tensor")),
        check_vma=False,
    )
```

time: 386 us -> 142 us (0.37)
  waiting for transfers between devices: 264 us -> 12.3 us
  Pallas kernels: 0 us -> 85.5 us
  local copies, waits for them, and re-layouts: 45.1 us -> 5.83 us
  matrix products: 22 us -> 0.32 us
  between operations: 13.9 us -> 0.7 us
  other arithmetic: 10.8 us -> 0.93 us
  starting transfers between devices: 11.3 us -> 18.6 us
    all_gather x1 -> x0, waiting for transfers between devices: 134 us -> none  [side_by_side(): lax.all_gather(both, axis, axis=dim, tiled=True)]
    reduce_scatter x2 -> x0, waiting for transfers between devices: 122 us -> none  [own_block(): pieces = lax.psum_scatter(pieces, axes[k], scatter_dimension=0, tiled=True)]
    pallas_call x0 -> x1, Pallas kernels: none -> 85.5 us  [fused(): pl.pallas_call(functools.partial(kernel, n_corpus // npass, scale_in, sca...]
    dot_general x7 -> x2, matrix products: 22 us -> 0.32 us  [the longest x1 0.19 us: local(): jnp.einsum('op,pd->od', pick.astype(BF16), embedding, preferred_element_t...]
    psum x0 -> x2, blocking collectives: none -> 18 us  [the longest x1 13.4 us: local(): squared = lax.psum(jnp.sum(pooled * pooled, axis=1), 'tensor')]
    all_to_all x1 -> x0, blocking collectives: 17 us -> none  [local(): lax.all_to_all(outbox, GROUP_DP, split_axis=0, concat_axis=0, tiled=True)]
    another operation x3 -> x0, local copies, waits for them, and re-layouts: 14.8 us -> none  [the longest x1 12.6 us: own_block(): pieces = pieces.reshape(*(lax.axis_size(a) for a in axes), *inside)]
    unnamed x21 -> x9, local copies, waits for them, and re-layouts: 19.1 us -> 4.37 us
  transfers between devices with their start and end apart: 6 -> 2, of which waited for: 5 -> 2; matrix products, arithmetic and copies ran while one was open for 3% -> 1% of each run, Pallas kernels for 0% -> 0%
where the time goes in v1:
time: 142 us
  Pallas kernels  85.5 us (60%)
  starting transfers between devices  18.6 us (13%)
  blocking collectives  18 us (13%)
  waiting for transfers between devices  12.3 us (9%)
  local copies, waits for them, and re-layouts  5.83 us (4%)
    pallas_call x1, Pallas kernels, fused(): pl.pallas_call(functools.partial(kernel, n_corpus // npass, scale_in, sca...  85.5 us
    psum x1, blocking collectives, local(): squared = lax.psum(jnp.sum(pooled * pooled, axis=1), 'tensor')  13.4 us
    all_to_all x1, starting transfers between devices, local(): pieces = lax.all_to_all(pieces, 'tensor', 0, 0, tiled=True)  11.1 us
    all_to_all x1, waiting for transfers between devices, local(): lax.all_to_all(outbox[:, None], GROUP_DP, split_axis=0, concat_axis=0, ti...  8.6 us
    all_to_all x1, starting transfers between devices, local(): lax.all_to_all(outbox[:, None], GROUP_DP, split_axis=0, concat_axis=0, ti...  7.5 us
    psum x1, blocking collectives, local(): pooled_branch = lax.psum(jnp.sum(pieces, axis=0), 'group')  4.55 us
    unnamed x9, local copies, waits for them, and re-layouts  4.37 us
    all_to_all x1, waiting for transfers between devices, local(): pieces = lax.all_to_all(pieces, 'tensor', 0, 0, tiled=True)  3.71 us
  transfers between devices with their start and end apart: 2, of which 2 were waited for; matrix products, arithmetic and copies ran while one was open for 1% of the time, Pallas kernels for 0%

profile of v1, /device:TPU:1, one launch (start us, length us, event | category | flops | bytes accessed | tf_op | source)
XLA Modules:
  0.0 142.1 jit_solution(14306217963061163251)
XLA Ops:
  0.6 0.0 copy-start
  0.6 0.0 copy-start.1
  0.7 85.5 %shard_map.94 = (bf16[64,1024]{1,0:T(8,128)(2,1)}, bf16[64,1024]{1,0:T(8,128)(2,1)}, f32[8,2048]{1,0:T(8,128)}) custom-call(bf16[512,2048]{1,0:T(8,128)(2,1)} %tokens_ref.1, bf16[512,2048]{1,0:T(8,128)(2,1)} %upstream_ref.1, bf16[256,2048]{1,0:T(8,128)(2,1)} %corpus_ref.1, s32[8]{0:T(128)} %len_ref.1, bf16[64,1024]{1,0:T(8,128)(2,1)} %win_ref.1, ...), custom_call_target="tpu_custom_call" | custom-call | tf_op jit(solution)/shard_map/pallas_call | solution.py:383
  86.2 11.1 %all-to-all-start = ((f32[8,8,256]{2,1,0:T(8,128)}), f32[8,8,256]{2,1,0:T(8,128)S(1)}, u32[]{:S(2)}, u32[]{:S(2)}) async-start(f32[8,8,256]{2,1,0:T(8,128)} %bitcast.22), calls=%async_computation | async-start | bytes 131072 | tf_op jit(solution)/shard_map/all_to_all | solution.py:451
  97.2 0.0 copy-done
  97.2 0.1 fusion.6
  97.3 0.9 constant_dynamic-slice_fusion
  98.2 0.1 fusion.1
  98.4 3.7 %all-to-all-done = f32[8,8,256]{2,1,0:T(8,128)S(1)} async-done(((f32[8,8,256]{2,1,0:T(8,128)}), f32[8,8,256]{2,1,0:T(8,128)S(1)}, u32[]{:S(2)}, u32[]{:S(2)}) %all-to-all-start) | async-done | bytes 65568 | tf_op jit(solution)/shard_map/all_to_all | solution.py:451
  102.1 4.6 %psum.14 = f32[8,256]{1,0:T(8,128)S(1)} all-reduce(f32[8,256]{1,0:T(8,128)S(1)} %reduce_sum.18), channel_id=1, replica_groups=mesh['group'=2,'dp_0'=2,'dp_1'=8,'tensor'=8] {'group'}, use_global_device_ids=true, to_apply=%region_1.0 | all-reduce | flops 2048 | bytes 16384 | tf_op jit(solution)/shard_map/psum | solution.py:452
  106.7 0.2 multiply_reduce_fusion
  106.8 13.4 %psum.15 = f32[8]{0:T(128)S(1)} all-reduce(f32[8]{0:T(128)S(1)} %multiply_reduce_fusion), channel_id=1, replica_groups=mesh['group'=2,'dp_0'=2,'dp_1'=8,'tensor'=8] {'tensor'}, use_global_device_ids=true, to_apply=%region_3.0 | all-reduce | flops 8 | bytes 64 | tf_op jit(solution)/shard_map/psum | solution.py:454
  120.3 0.0 copy-done.1
  120.3 0.2 fusion
  120.5 0.5 broadcast.20
  121.0 0.7 reduce
  121.6 0.6 reshape.24
  122.3 7.5 %all-to-all-start.1 = ((bf16[32,2,128]{2,1,0:T(2,128)(2,1)}), bf16[32,2,128]{2,1,0:T(2,128)(2,1)S(1)}, u32[]{:S(2)}, u32[]{:S(2)}) async-start(bf16[32,2,128]{2,1,0:T(2,128)(2,1)} %reshape.24), calls=%async_computation.1 | async-start | bytes 32768 | tf_op jit(solution)/shard_map/all_to_all | solution.py:461
  129.8 8.6 %all-to-all-done.1 = bf16[32,2,128]{2,1,0:T(2,128)(2,1)S(1)} async-done(((bf16[32,2,128]{2,1,0:T(2,128)(2,1)}), bf16[32,2,128]{2,1,0:T(2,128)(2,1)S(1)}, u32[]{:S(2)}, u32[]{:S(2)}) %all-to-all-start.1) | async-done | bytes 16416 | tf_op jit(solution)/shard_map/all_to_all | solution.py:461
  138.4 0.6 copy.27
  139.0 1.6 %copy.31 = bf16[64,1024]{1,0:T(8,128)(2,1)} copy(bf16[64,1024]{1,0:T(8,128)(2,1)} %get-tuple-element.12) | data formatting | bytes 262144
  140.6 1.6 %copy.32 = bf16[64,1024]{1,0:T(8,128)(2,1)} copy(bf16[64,1024]{1,0:T(8,128)(2,1)} %get-tuple-element.13) | data formatting | bytes 262144
  (5 shorter events, 0.1 us)
Async XLA Ops:
  0.6 96.6 %copy-start = (s32[8]{0:T(128)S(1)}, s32[8]{0:T(128)}, u32[]{:S(2)}) copy-start(s32[8]{0:T(128)} %len_ref.1) | copy-start | bytes 100
  0.6 119.6 %copy-start.1 = (s32[8]{0:T(128)S(1)}, s32[8]{0:T(128)}, u32[]{:S(2)}) copy-start(s32[8]{0:T(128)} %param.11) | copy-start | bytes 100
  86.2 15.9 %all-to-all-start = ((f32[8,8,256]{2,1,0:T(8,128)}), f32[8,8,256]{2,1,0:T(8,128)S(1)}, u32[]{:S(2)}, u32[]{:S(2)}) async-start(f32[8,8,256]{2,1,0:T(8,128)} %bitcast.22), calls=%async_computation | async-start | bytes 131072 | tf_op jit(solution)/shard_map/all_to_all | solution.py:451
  122.3 16.1 %all-to-all-start.1 = ((bf16[32,2,128]{2,1,0:T(2,128)(2,1)}), bf16[32,2,128]{2,1,0:T(2,128)(2,1)S(1)}, u32[]{:S(2)}, u32[]{:S(2)}) async-start(bf16[32,2,128]{2,1,0:T(2,128)(2,1)} %reshape.24), calls=%async_computation.1 | async-start | bytes 32768 | tf_op jit(solution)/shard_map/all_to_all | solution.py:461

commit v2 on v1

--- a/solution.py
+++ b/solution.py
@@ -19,6 +19,7 @@
 F32 = jnp.float32
 BF16 = jnp.bfloat16
 NZ = 8
+NT = 8
 
 
 def kernel(
@@ -29,11 +30,12 @@
     upstream_ref,
     corpus_ref,
     len_ref,
+    owner_ref,
     win_ref,
     wout_ref,
     new_in_ref,
     new_out_ref,
-    pool_ref,
+    index_ref,
     tok,
     up,
     cor,
@@ -53,6 +55,12 @@
     c_in,
     fin,
     land,
+    pool,
+    pool_in,
+    square,
+    square_in,
+    letter,
+    letter_in,
     lsem,
     ssem,
     rsem,
@@ -70,6 +78,10 @@
     zup = (g, yh, lax.rem(z + 1, NZ), t)
     zdn = (g, yh, lax.rem(z + NZ - 1, NZ), t)
     ring = (zup, zdn)
+
+    def cell(dg, dt):
+        return (lax.rem(g + dg, 2), yh, z, lax.rem(t + dt, NT))
+
     step_of = (1, -1)
 
     def at(k):
@@ -121,9 +133,11 @@
         loads.append(copy)
 
     barrier = pltpu.get_barrier_semaphore()
-    for device in (swap, mate, diag, zup, zdn):
+    met = [swap, mate, diag, zup, zdn]
+    met += [cell(dg, dt) for dg in range(2) for dt in range(1, NT)]
+    for device in met:
         pl.semaphore_signal(barrier, inc=1, device_id=device, device_id_type=MESH)
-    pl.semaphore_wait(barrier, 5)
+    pl.semaphore_wait(barrier, len(met))
 
     a0 = push(win_ref.at[:, own_cols], w_in.at[g, yh, z], mate)
     a1 = push(win_ref.at[:, other_cols], w_in.at[g, yh, z], swap)
@@ -295,6 +309,101 @@
                 o = 2 * pairs[j] + zz
                 g_out[gg, yh, o] = add(g_out[gg, yh, o], c_out[j - 1, gg, zz])
 
+    passages = len_ref.shape[0]
+    rows_c = cor.shape[0]
+    feat = pool.shape[-1]
+    mine = pl.ds(pl.multiple_of(t * feat, feat), feat)
+
+    def per_passage(ref, shape):
+        row = lax.broadcasted_iota(jnp.int32, shape, 0)
+        out = jnp.zeros(shape, jnp.int32)
+        for i in range(passages):
+            out = jnp.where(row == i, ref[i], out)
+        return out
+
+    def pool_rows():
+        pre = acc_c[...] * scale_in
+        cdf, _ = gelu_parts(pre)
+        ch = (pre * cdf).astype(BF16)
+        shape = (passages, rows_c)
+        row = lax.broadcasted_iota(jnp.int32, shape, 0)
+        col = lax.broadcasted_iota(jnp.int32, shape, 1)
+        lens = per_passage(len_ref, shape)
+        inside = jnp.logical_and(col >= row * plen, col < row * plen + lens)
+        live = jnp.where(inside, 1.0, 0.0).astype(BF16)
+        ph = jnp.dot(live, ch, preferred_element_type=F32)
+        hi = ph.astype(BF16)
+        lo = (ph - hi.astype(F32)).astype(BF16)
+        hl = jnp.concatenate([hi.astype(F32), lo.astype(F32)], axis=0).astype(BF16)
+
+        def branch(q, carry):
+            w = w_out[q // 2, lax.rem(q, 2)].reshape(NZ * shard, half)
+            both = lax.dot_general(hl, w, (((1,), (1,)), ((), ())), preferred_element_type=F32)
+            both = (both[:passages] + both[passages:]) * scale_out
+            for k in range(NZ * shard // feat):
+                pool[q * (NZ * shard // feat) + k] = both[:, k * feat : (k + 1) * feat]
+            return carry
+
+        lax.fori_loop(0, 4, branch, 0)
+        base = jnp.dot(live, cor[:, mine], preferred_element_type=F32)
+        copies = []
+        for dg in range(2):
+            for dt in range(NT):
+                if dg or dt:
+                    src = pool.at[lax.rem(t + dt, NT)]
+                    copies.append(push(src, pool_in.at[dg * NT + dt], cell(dg, dt)))
+        return base, copies
+
+    def square_rows(base, copies):
+        total = base + pool[t]
+        for copy in copies:
+            copy.wait_recv()
+        for k in range(1, 2 * NT):
+            total = total + pool_in[k]
+        lens = per_passage(len_ref, total.shape)
+        pooled = total * (1.0 / lens.astype(F32))
+        own_square = jnp.sum(pooled * pooled, axis=1, keepdims=True)
+        square[...] = jnp.broadcast_to(own_square, square.shape)
+        copies = [push(square, square_in.at[dt], cell(0, dt)) for dt in range(1, NT)]
+        return pooled, own_square, copies
+
+    def post_rows(pooled, own_square, copies):
+        for copy in copies:
+            copy.wait_recv()
+        total = own_square
+        for dt in range(1, NT):
+            total = total + square_in[dt][:, :1]
+        rows = pooled * lax.rsqrt(total / (NT * feat) + EPSILON)
+        owners = per_passage(owner_ref, rows.shape)
+        copies = []
+        for a in range(2):
+            for b in range(NZ):
+                to_yh, to_z = lax.rem(yh + a, 2), at(b)
+                owner = (g * 2 + to_yh) * NZ + to_z
+                row = jnp.sum(jnp.where(owners == owner, rows, 0.0), axis=0, keepdims=True)
+                if a or b:
+                    letter[a * NZ + b] = row
+                    copies.append(
+                        push(
+                            letter.at[a * NZ + b],
+                            letter_in.at[yh * NZ + z],
+                            (g, to_yh, to_z, t),
+                        )
+                    )
+                else:
+                    letter_in[yh * NZ + z] = row
+        return copies
+
+    def read_rows(copies):
+        for copy in copies:
+            copy.wait_recv()
+        row = lax.broadcasted_iota(jnp.int32, index_ref.shape, 0)
+        out = jnp.zeros(index_ref.shape, F32)
+        for d in range(2 * NZ):
+            out = jnp.where(row == d, jnp.broadcast_to(letter_in[d], out.shape), out)
+        index_ref[...] = out.astype(BF16)
+
+    stage = None
     for s in range(1, 5):
         j = 5 - s
         gradient(tok, dpre, g_in, scale_in, pairs[j])
@@ -306,31 +415,12 @@
             from_mate(j + 1)
             for d in range(2):
                 return_out(s - 1, d)
-
-    passages = pool_ref.shape[0]
-    rows_c = cor.shape[0]
-    cdf, _ = gelu_parts(acc_c[...] * scale_in)
-    ch = (acc_c[...] * scale_in * cdf).astype(BF16)
-    row = lax.broadcasted_iota(jnp.int32, (passages, rows_c), 0)
-    col = lax.broadcasted_iota(jnp.int32, (passages, rows_c), 1)
-    lens = jnp.zeros((passages, rows_c), jnp.int32)
-    for i in range(passages):
-        lens = jnp.where(row == i, len_ref[i], lens)
-    inside = jnp.logical_and(col >= row * plen, col < row * plen + lens)
-    live = jnp.where(inside, 1.0, 0.0).astype(BF16)
-    ph = jnp.dot(live, ch, preferred_element_type=F32)
-    hi = ph.astype(BF16)
-    lo = (ph - hi.astype(F32)).astype(BF16)
-    hl = jnp.concatenate([hi.astype(F32), lo.astype(F32)], axis=0).astype(BF16)
-
-    def branch(q, carry):
-        w = w_out[q // 2, lax.rem(q, 2)].reshape(NZ * shard, half)
-        both = lax.dot_general(hl, w, (((1,), (1,)), ((), ())), preferred_element_type=F32)
-        cols = pl.ds(pl.multiple_of(q * NZ * shard, NZ * shard), NZ * shard)
-        pool_ref[:, cols] = (both[:passages] + both[passages:]) * scale_out
-        return carry
-
-    lax.fori_loop(0, 4, branch, 0)
+        if s == 1:
+            stage = pool_rows()
+        elif s == 2:
+            stage = square_rows(*stage)
+        elif s == 3:
+            stage = post_rows(*stage)
 
     from_mate(1)
     for d in range(2):
@@ -366,18 +456,20 @@
     new_out_ref[:, other_cols] = land[1]
     home_in.wait_recv()
     new_in_ref[:, other_cols] = land[0]
+    read_rows(stage)
     for copy in sent:
         copy.wait_send()
 
 
-def fused(tokens, upstream, corpus, lengths, w_in, w_out, scale_in, scale_out):
+def fused(tokens, upstream, corpus, lengths, owners, w_in, w_out, scale_in, scale_out):
     shard, local_ff = w_in.shape
     half = local_ff // 2
     n_tok, width = tokens.shape
     n_corpus = corpus.shape[0]
     npass = lengths.shape[0]
     full = (2, 2, NZ, shard, half)
-    n_sem = 64
+    n_sem = 96
+    feat = width // NT
     any_spec = pl.BlockSpec(memory_space=pl.ANY)
     vmem_spec = pl.BlockSpec(memory_space=pltpu.VMEM)
     return pl.pallas_call(
@@ -385,12 +477,13 @@
         out_shape=(
             jax.ShapeDtypeStruct((shard, local_ff), BF16),
             jax.ShapeDtypeStruct((shard, local_ff), BF16),
-            jax.ShapeDtypeStruct((npass, width), F32),
+            jax.ShapeDtypeStruct((2 * NZ, feat), BF16),
         ),
         in_specs=[
             any_spec,
             any_spec,
             any_spec,
+            pl.BlockSpec(memory_space=pltpu.SMEM),
             pl.BlockSpec(memory_space=pltpu.SMEM),
             any_spec,
             any_spec,
@@ -416,6 +509,12 @@
             pltpu.VMEM((2, shard, half), BF16),
             pltpu.VMEM((2, 2, shard, half), BF16),
             pltpu.VMEM((2, shard, half), BF16),
+            pltpu.VMEM((NT, npass, feat), F32),
+            pltpu.VMEM((2 * NT, npass, feat), F32),
+            pltpu.VMEM((npass, 128), F32),
+            pltpu.VMEM((NT, npass, 128), F32),
+            pltpu.VMEM((2 * NZ, 1, feat), F32),
+            pltpu.VMEM((2 * NZ, 1, feat), F32),
             pltpu.SemaphoreType.DMA((5,)),
             pltpu.SemaphoreType.DMA((n_sem,)),
             pltpu.SemaphoreType.DMA((n_sem,)),
@@ -423,7 +522,7 @@
         compiler_params=pltpu.CompilerParams(
             collective_id=0, has_side_effects=True, vmem_limit_bytes=60 * 1024 * 1024
         ),
-    )(tokens, upstream, corpus, lengths, w_in, w_out)
+    )(tokens, upstream, corpus, lengths, owners, w_in, w_out)
 
 
 def local(tokens, upstream, corpus, lengths, owners, w_in, w_out):
@@ -434,33 +533,7 @@
     width = shard_rows * groups * replicas
     scale_in = 1.0 / math.sqrt(width)
     scale_out = 1.0 / math.sqrt(local_ff * lax.axis_size("tensor"))
-    cols = width // lax.axis_size("tensor")
-    n_corpus = corpus.shape[0]
-    npass = lengths.shape[0]
-    plen = n_corpus // npass
-    owner_count = groups * replicas
-    new_in, new_out, partial_pool = fused(
-        tokens, upstream, corpus, lengths, w_in, w_out, scale_in, scale_out
-    )
-    live = jnp.arange(plen, dtype=jnp.int32)[None, :] < lengths[:, None]
-    own_cols = lax.dynamic_slice_in_dim(corpus, lax.axis_index("tensor") * cols, cols, 1).reshape(
-        npass, plen, cols
-    )
-    base = jnp.einsum("pl,pld->pd", live.astype(BF16), own_cols, preferred_element_type=F32)
-    pieces = partial_pool.reshape(npass, -1, cols).transpose(1, 0, 2)
-    pieces = lax.all_to_all(pieces, "tensor", 0, 0, tiled=True)
-    pooled_branch = lax.psum(jnp.sum(pieces, axis=0), "group")
-    pooled = (base + pooled_branch) * (1.0 / lengths.astype(F32))[:, None]
-    squared = lax.psum(jnp.sum(pooled * pooled, axis=1), "tensor")
-    embedding = (pooled * lax.rsqrt(squared / width + EPSILON)[:, None]).astype(BF16)
-    owner_ids = jnp.arange(owner_count, dtype=jnp.int32)
-    pick = owners[None, :] == owner_ids[:, None]
-    outbox = jnp.einsum(
-        "op,pd->od", pick.astype(BF16), embedding, preferred_element_type=F32
-    ).astype(BF16)
-    inbox = lax.all_to_all(outbox[:, None], GROUP_DP, split_axis=0, concat_axis=0, tiled=True)
-    index_rows = inbox[:replicas].reshape(replicas, cols)
-    return (new_in, new_out, index_rows)
+    return fused(tokens, upstream, corpus, lengths, owners, w_in, w_out, scale_in, scale_out)
 
 
 def solution(mesh):

time: 142 us -> 102 us (0.72)
  the two profiles are of different devices: /device:TPU:1 before, /device:TPU:14 now
where the time goes in v2:
time: 102 us
  Pallas kernels  96.8 us (95%)
  local copies, waits for them, and re-layouts  4.43 us (4%)
    pallas_call x1, Pallas kernels, fused(): pl.pallas_call(functools.partial(kernel, n_corpus // npass, scale_in, sca...  96.8 us
    unnamed x3, local copies, waits for them, and re-layouts  4.43 us

profile of v2, /device:TPU:14, one launch (start us, length us, event | category | flops | bytes accessed | tf_op | source)
XLA Modules:
  0.0 101.9 jit_solution(2846902637468373265)
XLA Ops:
  0.6 96.8 %shard_map.94 = (bf16[64,1024]{1,0:T(8,128)(2,1)}, bf16[64,1024]{1,0:T(8,128)(2,1)}, bf16[16,256]{1,0:T(8,128)(2,1)}) custom-call(bf16[512,2048]{1,0:T(8,128)(2,1)} %tokens_ref.1, bf16[512,2048]{1,0:T(8,128)(2,1)} %upstream_ref.1, bf16[256,2048]{1,0:T(8,128)(2,1)} %corpus_ref.1, s32[8]{0:T(128)} %len_ref.1, s32[8]{0:T(128)} %owner_ref.1, ...), custom_call_target="tpu_custom_call" | custom-call | tf_op jit(solution)/shard_map/pallas_call | solution.py:475
  97.5 1.6 %copy.13 = bf16[64,1024]{1,0:T(8,128)(2,1)} copy(bf16[64,1024]{1,0:T(8,128)(2,1)} %get-tuple-element.6) | data formatting | bytes 262144
  99.0 1.6 %copy.14 = bf16[64,1024]{1,0:T(8,128)(2,1)} copy(bf16[64,1024]{1,0:T(8,128)(2,1)} %get-tuple-element.7) | data formatting | bytes 262144
  100.6 1.3 %copy.15 = bf16[16,256]{1,0:T(8,128)(2,1)} copy(bf16[16,256]{1,0:T(8,128)(2,1)} %get-tuple-element.8) | data formatting | bytes 16384

commit v3 on v2

v3 whole, which is shorter than its diff:
```python
import functools
import math

import jax
import jax.numpy as jnp
from jax import lax
from jax.experimental import pallas as pl
from jax.experimental.pallas import tpu as pltpu
from jax.sharding import Mesh
from jax.sharding import PartitionSpec as P

DP = ("dp_0", "dp_1")
GROUP_DP = ("group", "dp_0", "dp_1")
MESH = pl.DeviceIdType.MESH

LEARN_RATE = 0.5
EPSILON = 1e-06
F32 = jnp.float32
BF16 = jnp.bfloat16
NZ = 8
NT = 8
TURNS = ((1, 1), (1, 0), (0, 1))


def kernel(
    plen,
    scale_in,
    scale_out,
    tokens_ref,
    upstream_ref,
    corpus_ref,
    len_ref,
    owner_ref,
    win_ref,
    wout_ref,
    new_in_ref,
    new_out_ref,
    index_ref,
    tok,
    up,
    cor,
    w_in,
    w_out,
    acc_p,
    acc_d,
    acc_c,
    hid,
    dpre,
    g_in,
    g_out,
    r_in,
    r_out,
    fin,
    land,
    lens_here,
    lens_there,
    pool,
    pool_in,
    square,
    square_in,
    letter,
    letter_in,
    lsem,
    ssem,
    rsem,
):
    g = lax.axis_index("group")
    yh = lax.axis_index("dp_0")
    z = lax.axis_index("dp_1")
    t = lax.axis_index("tensor")
    core = lax.rem(t, 2)
    par = lax.rem(t // 2, 2)
    cut = w_in.shape[-1]
    shard = w_in.shape[-2]

    def cell(dg, dy, dt):
        return (lax.rem(g + dg, 2), lax.rem(yh + dy, 2), z, lax.rem(t + dt, NT))

    def column(dg, dy):
        return cell(dg, dy, 0)

    twin = (g, yh, z, t + 1 - 2 * core)
    right, left = cell(0, 0, 2), cell(0, 0, NT - 2)
    mate, swap = column(1, 1), column(1, 0)
    ring = (
        (g, yh, lax.rem(z + 1, NZ), t),
        (g, yh, lax.rem(z + NZ - 1, NZ), t),
    )
    step_of = (1, -1)

    def at(k):
        return lax.rem(z + k + 2 * NZ, NZ)

    barrier = pltpu.get_barrier_semaphore()
    met = [column(dg, dy) for dg, dy in TURNS] + list(ring) + [twin, right, left]
    met += [cell(0, 0, 4)] + [cell(dg, dy, 4) for dg, dy in TURNS]
    for device in met:
        pl.semaphore_signal(barrier, inc=1, device_id=device, device_id_type=MESH)

    def cols_of(dg, dy):
        q = lax.rem(g + dg, 2) * 2 + lax.rem(yh + dy, 2)
        return pl.ds(pl.multiple_of(q * cut, cut), cut)

    own_cols = cols_of(0, 0)
    groups_of_half = tok.shape[0] // 2
    here = pl.ds(yh * groups_of_half, groups_of_half)
    loads = []
    for k, (src, dst) in enumerate(
        (
            (win_ref.at[:, own_cols], w_in.at[g, yh, z]),
            (wout_ref.at[:, own_cols], w_out.at[g, yh, z]),
            (tokens_ref, tok.at[here]),
            (corpus_ref, cor.at[here]),
            (upstream_ref, up.at[here]),
        )
    ):
        copy = pltpu.make_async_copy(src, dst, lsem.at[k])
        copy.start()
        loads.append(copy)

    passages = len_ref.shape[0]

    def per_passage(ref, shape):
        row = lax.broadcasted_iota(jnp.int32, shape, 0)
        out = jnp.zeros(shape, jnp.int32)
        for i in range(passages):
            out = jnp.where(row == i, ref[i], out)
        return out

    lens_here[...] = per_passage(len_ref, lens_here.shape)

    half_nz = NZ // 2
    pair = z // 2
    e = 1 - 2 * lax.rem(z, 2)
    pairs = (
        None,
        pair,
        lax.rem(pair - e + half_nz, half_nz),
        lax.rem(pair + e + half_nz, half_nz),
        lax.rem(pair + 2, half_nz),
    )

    count = [0]
    sent = []

    def push(src, dst, device):
        k = count[0]
        count[0] += 1
        copy = pltpu.make_async_remote_copy(
            src_ref=src,
            dst_ref=dst,
            send_sem=ssem.at[k],
            recv_sem=rsem.at[k],
            device_id=device,
            device_id_type=MESH,
        )
        copy.start()
        sent.append(copy)
        return copy

    def same(ref, device):
        return push(ref, ref, device)

    pl.semaphore_wait(barrier, len(met))

    weights = ((win_ref, w_in), (wout_ref, w_out))
    first = [[[] for _ in range(2)] for _ in range(2)]
    for a, (src, w) in enumerate(weights):
        for d in range(2):
            first[a][d].append(push(src.at[:, own_cols], w.at[g, yh, z], ring[d]))
    slices = [[], []]
    for a, (src, w) in enumerate(weights):
        for dg, dy in TURNS:
            slices[a].append(push(src.at[:, cols_of(dg, dy)], w.at[g, yh, z], column(dg, dy)))

    def part(half, h, who=core):
        return pl.ds(half * groups_of_half + who * 4 + h * 2, 2)

    there = 1 - yh
    arrays = ((tokens_ref, tok), (upstream_ref, up), (corpus_ref, cor))
    from_mate = []
    for src, buf in arrays:
        given = pl.ds(core * 4 + (1 - g) * 2, 2)
        from_mate.append(push(src.at[given, par], buf.at[part(yh, 1 - g), par], mate))
    lens_copy = push(lens_here, lens_there, mate)
    from_swap = [None] * 3
    from_side = [[] for _ in range(3)]
    from_twin = [[] for _ in range(3)]

    def sideways(k, h):
        buf = arrays[k][1]
        start = there * groups_of_half + core * 4 + h * 2
        from_side[k].append(same(buf.at[pl.ds(start + 1, 1), par], right))
        from_side[k].append(same(buf.at[pl.ds(start, 1), par], left))

    def after_mate(k):
        buf = arrays[k][1]
        from_mate[k].wait_recv()
        from_swap[k] = same(buf.at[part(there, g), par], swap)
        sideways(k, g)
        from_twin[k].append(same(buf.at[part(there, g), par], twin))

    def after_swap(k):
        buf = arrays[k][1]
        from_swap[k].wait_recv()
        sideways(k, 1 - g)
        from_twin[k].append(same(buf.at[part(there, 1 - g), par], twin))

    def after_side(k):
        buf = arrays[k][1]
        for i, h in enumerate((g, 1 - g)):
            from_side[k][2 * i].wait_recv()
            from_side[k][2 * i + 1].wait_recv()
            from_twin[k].append(same(buf.at[part(there, h), 1 - par], twin))

    def after_twin(k):
        for copy in from_twin[k]:
            copy.wait_recv()

    loads[0].wait()
    loads[1].wait()
    for a, (_, w) in enumerate(weights):
        for i, (dg, dy) in enumerate(TURNS):
            slices[a][i].wait_recv()
            block = w.at[lax.rem(g + dg, 2), lax.rem(yh + dy, 2), z]
            for d in range(2):
                first[a][d].append(same(block, ring[d]))

    def send_ring(a, s, d):
        w = weights[a][1]
        o = at(-step_of[d] * (s - 1))
        return same(w.at[:, :, o] if s < 4 else w.at[d, :, o], ring[d])

    def rows_of(x, base, tile, p):
        parts = []
        per = x.shape[1] * x.shape[2]
        for q in range(4):
            at_q = pl.multiple_of(q * NZ * shard + p * 2 * shard, 2 * shard)
            block = x[pl.ds(base, tile // per), :, :, pl.ds(at_q, 2 * shard)]
            parts.append(block.reshape(tile, 2 * shard))
        return jnp.concatenate(parts, axis=1)

    def weight(w, p):
        parts = []
        for q in range(4):
            block = w[q // 2, q % 2, pl.ds(2 * p, 2)]
            parts.append(block.reshape(2 * shard, cut))
        return jnp.concatenate(parts, axis=0)

    def multiply(x, w, acc, half, p, is_first):
        per = x.shape[1] * x.shape[2]
        tile = 256
        rows_half = per * groups_of_half

        def body(m, carry):
            base = half * groups_of_half + m * (tile // per)
            rows = pl.ds(pl.multiple_of(half * rows_half + m * tile, tile), tile)
            part_sum = jnp.dot(rows_of(x, base, tile, p), weight(w, p), preferred_element_type=F32)
            acc[rows, :] = part_sum if is_first else acc[rows, :] + part_sum
            return carry

        lax.fori_loop(0, rows_half // tile, body, 0)

    got = [[[None] * 2 for _ in range(5)] for _ in range(2)]
    after_mate(0)
    for s in range(1, 5):
        for a in range(2):
            for d in range(2):
                if s == 1:
                    for copy in first[a][d]:
                        copy.wait_recv()
                else:
                    got[a][s][d].wait_recv()
                if s < 4:
                    got[a][s + 1][d] = send_ring(a, s + 1, d)
        if s == 1:
            after_swap(0)
            after_mate(1)
            loads[2].wait()
            loads[4].wait()
        elif s == 2:
            after_side(0)
            after_swap(1)
            after_mate(2)
        elif s == 3:
            after_side(1)
            after_swap(2)
            after_twin(0)
        multiply(tok, w_in, acc_p, yh, pairs[s], s == 1)
        multiply(up, w_out, acc_d, yh, pairs[s], s == 1)
        if s == 3:
            for k in range(1, 4):
                multiply(tok, w_in, acc_p, there, pairs[k], k == 1)
    after_side(2)
    multiply(tok, w_in, acc_p, there, pairs[4], False)
    after_twin(1)
    for k in range(1, 5):
        multiply(up, w_out, acc_d, there, pairs[k], k == 1)

    root = math.sqrt(2.0 / math.pi)

    def gelu_parts(p):
        th = jnp.tanh(root * (p + 0.044715 * (p * p * p)))
        return 0.5 * (1.0 + th), th

    slab = 64

    def activate(m, carry):
        rows = pl.ds(pl.multiple_of(m * slab, slab), slab)
        p = acc_p[rows, :] * scale_in
        dh = acc_d[rows, :] * scale_out
        cdf, th = gelu_parts(p)
        hid[rows, :] = (p * cdf).astype(BF16)
        slope = cdf + (0.5 * root) * p * (1.0 - th * th) * (1.0 + (3 * 0.044715) * (p * p))
        dpre[rows, :] = (dh * slope).astype(BF16)
        return carry

    n_tok = acc_p.shape[0]
    lax.fori_loop(0, n_tok // slab, activate, 0)

    def gradient(x, y, out, scale, p):
        def body(gg, carry):
            parts = []
            for yy in range(2):
                at_q = pl.multiple_of((gg * 2 + yy) * NZ * shard + p * 2 * shard, 2 * shard)
                block = x[:, :, :, pl.ds(at_q, 2 * shard)]
                parts.append(block.reshape(n_tok, 2 * shard))
            both = lax.dot_general(
                jnp.concatenate(parts, axis=1),
                y[...],
                (((0,), (0,)), ((), ())),
                preferred_element_type=F32,
            )
            both = (both * scale).astype(BF16).reshape(2, 2, shard, cut)
            for yy in range(2):
                out[gg, yy, pl.ds(2 * p, 2)] = both[yy]
            return carry

        lax.fori_loop(0, 2, body, 0)

    def add(a, b):
        return (a.astype(F32) + b.astype(F32)).astype(BF16)

    back = [[[None] * 2 for _ in range(5)] for _ in range(2)]

    def give_back(a, s, d):
        grad, arrived = ((g_in, r_in), (g_out, r_out))[a]
        o = at(step_of[d] * (5 - s))
        if s == 1:
            back[a][1][d] = push(grad.at[d, :, o], arrived.at[d, 0, d], ring[d])
            return
        back[a][s - 1][d].wait_recv()
        if s == 2:
            for yy in range(2):
                grad[d, yy, o] = add(grad[d, yy, o], arrived[d, 0, d, yy])
        else:
            for gg in range(2):
                for yy in range(2):
                    grad[gg, yy, o] = add(grad[gg, yy, o], arrived[d, s - 2, gg, yy])
        back[a][s][d] = push(grad.at[:, :, o], arrived.at[d, s - 1], ring[d])

    feat = pool.shape[-1]
    rows_c = acc_c.shape[0] // 2
    mine = pl.ds(pl.multiple_of(t * feat, feat), feat)

    def pool_rows():
        after_twin(2)
        lens_copy.wait_recv()
        loads[3].wait()
        for half in (yh, there):
            for k in range(1, 5):
                multiply(cor, w_in, acc_c, half, pairs[k], k == 1)
        shape = (passages, rows_c)
        row = lax.broadcasted_iota(jnp.int32, shape, 0)
        col = lax.broadcasted_iota(jnp.int32, shape, 1)
        stack = []
        for half, lens in ((yh, lens_here), (there, lens_there)):
            span = pl.ds(pl.multiple_of(half * rows_c, rows_c), rows_c)
            pre = acc_c[span, :] * scale_in
            cdf, _ = gelu_parts(pre)
            ch = (pre * cdf).astype(BF16)
            stop = row * plen + jnp.broadcast_to(lens[:, :1], shape)
            inside = jnp.logical_and(col >= row * plen, col < stop)
            live = jnp.where(inside, 1.0, 0.0).astype(BF16)
            if not stack:
                x = cor[pl.ds(yh * groups_of_half, groups_of_half), :, :, mine]
                base = jnp.dot(live, x.reshape(rows_c, feat), preferred_element_type=F32)
            ph = jnp.dot(live, ch, preferred_element_type=F32)
            hi = ph.astype(BF16).astype(F32)
            stack += [hi, ph - hi]
        hl = jnp.concatenate(stack, axis=0).astype(BF16)

        def branch(q, carry):
            w = w_out[q // 2, lax.rem(q, 2)].reshape(NZ * shard, cut)
            both = lax.dot_general(hl, w, (((1,), (1,)), ((), ())), preferred_element_type=F32)
            both = both * scale_out
            n = NZ * shard // feat
            for i in range(2):
                rows = both[2 * i * passages : (2 * i + 1) * passages]
                rows = rows + both[(2 * i + 1) * passages : (2 * i + 2) * passages]
                for k in range(n):
                    pool[i, q * n + k] = rows[:, k * feat : (k + 1) * feat]
            return carry

        lax.fori_loop(0, 4, branch, 0)
        copies = []
        for dy in range(2):
            for dg in range(2):
                for dt in range(NT):
                    if dy or dg or dt:
                        src = pool.at[dy, lax.rem(t + dt, NT)]
                        slot = pool_in.at[(dy * 2 + dg) * NT + dt]
                        copies.append(push(src, slot, cell(dg, dy, dt)))
        return base, copies

    def square_rows(base, copies):
        total = base + pool[0, t]
        for copy in copies:
            copy.wait_recv()
        for k in range(1, 4 * NT):
            total = total + pool_in[k]
        lens = jnp.broadcast_to(lens_here[:, :1], total.shape)
        pooled = total * (1.0 / lens.astype(F32))
        own_square = jnp.sum(pooled * pooled, axis=1, keepdims=True)
        square[...] = jnp.broadcast_to(own_square, square.shape)
        copies = [push(square, square_in.at[dt], cell(0, 0, dt)) for dt in range(1, NT)]
        return pooled, own_square, copies

    def post_rows(pooled, own_square, copies):
        for copy in copies:
            copy.wait_recv()
        total = own_square
        for dt in range(1, NT):
            total = total + square_in[dt][:, :1]
        rows = pooled * lax.rsqrt(total / (NT * feat) + EPSILON)
        owners = per_passage(owner_ref, rows.shape)
        copies = []
        for a in range(2):
            for b in range(NZ):
                to_yh, to_z = lax.rem(yh + a, 2), at(b)
                owner = (g * 2 + to_yh) * NZ + to_z
                row = jnp.sum(jnp.where(owners == owner, rows, 0.0), axis=0, keepdims=True)
                if a or b:
                    letter[a * NZ + b] = row
                    copies.append(
                        push(
                            letter.at[a * NZ + b],
                            letter_in.at[yh * NZ + z],
                            (g, to_yh, to_z, t),
                        )
                    )
                else:
                    letter_in[yh * NZ + z] = row
        return copies

    def read_rows(copies):
        for copy in copies:
            copy.wait_recv()
        row = lax.broadcasted_iota(jnp.int32, index_ref.shape, 0)
        out = jnp.zeros(index_ref.shape, F32)
        for d in range(2 * NZ):
            out = jnp.where(row == d, jnp.broadcast_to(letter_in[d], out.shape), out)
        index_ref[...] = out.astype(BF16)

    stage = None
    for s in range(1, 5):
        p = pairs[5 - s]
        gradient(tok, dpre, g_in, scale_in, p)
        for d in range(2):
            give_back(0, s, d)
        gradient(up, hid, g_out, scale_out, p)
        for d in range(2):
            give_back(1, s, d)
        if s == 1:
            stage = pool_rows()
        elif s == 2:
            stage = square_rows(*stage)
        elif s == 3:
            stage = post_rows(*stage)

    home = [[], []]
    outs = (new_in_ref, new_out_ref)
    sums = ((g_in, r_in, w_in), (g_out, r_out, w_out))
    for a, (grad, arrived, w) in enumerate(sums):
        for d in range(2):
            back[a][4][d].wait_recv()
        for i, (dg, dy) in enumerate(TURNS + ((0, 0),)):
            gg, yy = lax.rem(g + dg, 2), lax.rem(yh + dy, 2)
            total = (
                grad[gg, yy, z].astype(F32)
                + arrived[0, 3, gg, yy].astype(F32)
                + arrived[1, 3, gg, yy].astype(F32)
            )
            new = (w[gg, yy, z].astype(F32) - LEARN_RATE * total).astype(BF16)
            if dg or dy:
                fin[a, i] = new
                home[a].append(push(fin.at[a, i], land.at[a, i], column(dg, dy)))
            else:
                outs[a][:, own_cols] = new
    read_rows(stage)
    for a in range(2):
        for i, (dg, dy) in enumerate(TURNS):
            home[a][i].wait_recv()
            outs[a][:, cols_of(dg, dy)] = land[a, i]
    for copy in sent:
        copy.wait_send()


def fused(tokens, upstream, corpus, lengths, owners, w_in, w_out, scale_in, scale_out):
    shard, local_ff = w_in.shape
    cut = local_ff // 4
    n_tok, width = tokens.shape
    n_corpus = corpus.shape[0]
    npass = lengths.shape[0]
    full = (2, 2, NZ, shard, cut)
    n_sem = 160
    feat = width // NT
    rows_t, rows_c = n_tok // 16, n_corpus // 16
    any_spec = pl.BlockSpec(memory_space=pl.ANY)
    vmem_spec = pl.BlockSpec(memory_space=pltpu.VMEM)
    smem_spec = pl.BlockSpec(memory_space=pltpu.SMEM)
    return pl.pallas_call(
        functools.partial(kernel, n_corpus // npass, scale_in, scale_out),
        out_shape=(
            jax.ShapeDtypeStruct((shard, local_ff), BF16),
            jax.ShapeDtypeStruct((shard, local_ff), BF16),
            jax.ShapeDtypeStruct((2 * NZ, feat), BF16),
        ),
        in_specs=[any_spec, any_spec, any_spec, smem_spec, smem_spec, any_spec, any_spec],
        out_specs=(vmem_spec, vmem_spec, vmem_spec),
        scratch_shapes=[
            pltpu.VMEM((16, 2, rows_t, width), BF16),
            pltpu.VMEM((16, 2, rows_t, width), BF16),
            pltpu.VMEM((16, 2, rows_c, width), BF16),
            pltpu.VMEM(full, BF16),
            pltpu.VMEM(full, BF16),
            pltpu.VMEM((2 * n_tok, cut), F32),
            pltpu.VMEM((2 * n_tok, cut), F32),
            pltpu.VMEM((2 * n_corpus, cut), F32),
            pltpu.VMEM((2 * n_tok, cut), BF16),
            pltpu.VMEM((2 * n_tok, cut), BF16),
            pltpu.VMEM(full, BF16),
            pltpu.VMEM(full, BF16),
            pltpu.VMEM((2, 4, 2, 2, shard, cut), BF16),
            pltpu.VMEM((2, 4, 2, 2, shard, cut), BF16),
            pltpu.VMEM((2, 3, shard, cut), BF16),
            pltpu.VMEM((2, 3, shard, cut), BF16),
            pltpu.VMEM((npass, 128), jnp.int32),
            pltpu.VMEM((npass, 128), jnp.int32),
            pltpu.VMEM((2, NT, npass, feat), F32),
            pltpu.VMEM((4 * NT, npass, feat), F32),
            pltpu.VMEM((npass, 128), F32),
            pltpu.VMEM((NT, npass, 128), F32),
            pltpu.VMEM((2 * NZ, 1, feat), F32),
            pltpu.VMEM((2 * NZ, 1, feat), F32),
            pltpu.SemaphoreType.DMA((5,)),
            pltpu.SemaphoreType.DMA((n_sem,)),
            pltpu.SemaphoreType.DMA((n_sem,)),
        ],
        compiler_params=pltpu.CompilerParams(
            collective_id=0, has_side_effects=True, vmem_limit_bytes=60 * 1024 * 1024
        ),
    )(
        tokens.reshape(8, 2, rows_t, width),
        upstream.reshape(8, 2, rows_t, width),
        corpus.reshape(8, 2, rows_c, width),
        lengths,
        owners,
        w_in,
        w_out,
    )


def local(tokens, upstream, corpus, lengths, owners, w_in, w_out):
    width = w_in.shape[0] * lax.axis_size(GROUP_DP)
    hidden_units = w_in.shape[1] * lax.axis_size("tensor")
    scale_in = 1.0 / math.sqrt(width)
    scale_out = 1.0 / math.sqrt(hidden_units)
    return fused(tokens, upstream, corpus, lengths, owners, w_in, w_out, scale_in, scale_out)


def solution(mesh):
    torus = Mesh(
        mesh.devices.reshape(mesh.shape["group"], 2, NZ, mesh.shape["tensor"]),
        ("group", "dp_0", "dp_1", "tensor"),
    )
    return jax.shard_map(
        local,
        mesh=torus,
        in_specs=(
            P(DP, None),
            P(DP, None),
            P(DP, None),
            P(DP),
            P(DP),
            P(GROUP_DP, "tensor"),
            P(GROUP_DP, "tensor"),
        ),
        out_specs=(P(GROUP_DP, "tensor"), P(GROUP_DP, "tensor"), P(GROUP_DP, "tensor")),
        check_vma=False,
    )
```

time: 102 us -> 83 us (0.81)
  the two profiles are of different devices: /device:TPU:14 before, /device:TPU:1 now
where the time goes in v3:
time: 83 us; the launch traced here: 82.8 us
  Pallas kernels  77.7 us (94%)
  local copies, waits for them, and re-layouts  4.43 us (5%)
    pallas_call x1, Pallas kernels, fused(): pl.pallas_call(functools.partial(kernel, n_corpus // npass, scale_in, sca...  77.7 us
    unnamed x3, local copies, waits for them, and re-layouts  4.43 us

profile of v3, /device:TPU:1, one launch (start us, length us, event | category | flops | bytes accessed | tf_op | source)
XLA Modules:
  0.0 82.8 jit_solution(12852766864162624559)
XLA Ops:
  0.6 77.7 %shard_map.94 = (bf16[64,1024]{1,0:T(8,128)(2,1)}, bf16[64,1024]{1,0:T(8,128)(2,1)}, bf16[16,256]{1,0:T(8,128)(2,1)}) custom-call(bf16[8,2,32,2048]{3,2,1,0:T(8,128)(2,1)} %bitcast.3, bf16[8,2,32,2048]{3,2,1,0:T(8,128)(2,1)} %bitcast.4, bf16[8,2,16,2048]{3,2,1,0:T(8,128)(2,1)} %bitcast.5, s32[8]{0:T(128)} %len_ref.1, s32[8]{0:T(128)} %owner_ref.1, ...), custom_call_target="tpu_custom_call" | custom-call | tf_op jit(solution)/shard_map/pallas_call | solution.py:522
  78.4 1.6 %copy.13 = bf16[64,1024]{1,0:T(8,128)(2,1)} copy(bf16[64,1024]{1,0:T(8,128)(2,1)} %get-tuple-element.6) | data formatting | bytes 262144
  79.9 1.6 %copy.14 = bf16[64,1024]{1,0:T(8,128)(2,1)} copy(bf16[64,1024]{1,0:T(8,128)(2,1)} %get-tuple-element.7) | data formatting | bytes 262144
  81.5 1.3 %copy.15 = bf16[16,256]{1,0:T(8,128)(2,1)} copy(bf16[16,256]{1,0:T(8,128)(2,1)} %get-tuple-element.8) | data formatting | bytes 16384

commit v4 on v3

v4 whole, which is shorter than its diff:
```python
import functools
import math

import jax
import jax.numpy as jnp
from jax import lax
from jax.experimental import pallas as pl
from jax.experimental.pallas import tpu as pltpu
from jax.sharding import Mesh
from jax.sharding import PartitionSpec as P

DP = ("dp_0", "dp_1")
GROUP_DP = ("group", "dp_0", "dp_1")
MESH = pl.DeviceIdType.MESH

LEARN_RATE = 0.5
EPSILON = 1e-06
F32 = jnp.float32
BF16 = jnp.bfloat16
NZ = 8
NT = 8
N_SEM = 91
TURNS = ((1, 1), (1, 0), (0, 1))


def kernel(
    plen,
    scale_in,
    scale_out,
    tokens_ref,
    upstream_ref,
    corpus_ref,
    len_hbm,
    owner_hbm,
    win_ref,
    wout_ref,
    new_in_ref,
    new_out_ref,
    index_ref,
    tok,
    up,
    cor,
    w_in,
    w_out,
    acc_p,
    acc_d,
    acc_c,
    hid,
    dpre,
    g_in,
    g_out,
    r_in,
    r_out,
    fin,
    lens_here,
    lens_there,
    pool,
    pool_in,
    square,
    square_in,
    letter,
    letter_in,
    len_ref,
    owner_ref,
    lsem,
    ssem,
    rsem,
):
    g = lax.axis_index("group")
    yh = lax.axis_index("dp_0")
    z = lax.axis_index("dp_1")
    t = lax.axis_index("tensor")
    core = lax.rem(t, 2)
    par = lax.rem(t // 2, 2)
    cut = w_in.shape[-1]
    shard = w_in.shape[-2]

    def cell(dg, dy, dt):
        return (lax.rem(g + dg, 2), lax.rem(yh + dy, 2), z, lax.rem(t + dt, NT))

    def column(dg, dy):
        return cell(dg, dy, 0)

    twin = (g, yh, z, t + 1 - 2 * core)
    right, left = cell(0, 0, 2), cell(0, 0, NT - 2)
    mate, swap = column(1, 1), column(1, 0)
    ring = (
        (g, yh, lax.rem(z + 1, NZ), t),
        (g, yh, lax.rem(z + NZ - 1, NZ), t),
    )
    step_of = (1, -1)

    def at(k):
        return lax.rem(z + k + 2 * NZ, NZ)

    barrier = pltpu.get_barrier_semaphore()
    met = [column(dg, dy) for dg, dy in TURNS] + list(ring) + [twin, right, left]
    met += [cell(0, 0, 4)] + [cell(dg, dy, 4) for dg, dy in TURNS]
    for device in met:
        pl.semaphore_signal(barrier, inc=1, device_id=device, device_id_type=MESH)

    def cols_of(dg, dy):
        q = lax.rem(g + dg, 2) * 2 + lax.rem(yh + dy, 2)
        return pl.ds(pl.multiple_of(q * cut, cut), cut)

    own_cols = cols_of(0, 0)
    groups_of_half = tok.shape[0] // 2
    here = pl.ds(yh * groups_of_half, groups_of_half)
    loads = []

    def load(src, dst):
        copy = pltpu.make_async_copy(src, dst, lsem.at[len(loads)])
        copy.start()
        loads.append(copy)
        return copy

    load_lens = load(len_hbm, len_ref)
    load_owners = load(owner_hbm, owner_ref)
    load_in = load(win_ref.at[:, own_cols], w_in.at[g, yh, z])
    load_out = load(wout_ref.at[:, own_cols], w_out.at[g, yh, z])
    load_tok = load(tokens_ref, tok.at[here])
    load_up = load(upstream_ref, up.at[here])
    load_cor = load(corpus_ref, cor.at[here])

    passages = len_ref.shape[0]

    def per_passage(ref, shape):
        row = lax.broadcasted_iota(jnp.int32, shape, 0)
        out = jnp.zeros(shape, jnp.int32)
        for i in range(passages):
            out = jnp.where(row == i, ref[i], out)
        return out

    half_nz = NZ // 2
    pair = z // 2
    e = 1 - 2 * lax.rem(z, 2)
    pairs = (
        None,
        pair,
        lax.rem(pair - e + half_nz, half_nz),
        lax.rem(pair + e + half_nz, half_nz),
        lax.rem(pair + 2, half_nz),
    )

    count = [0]

    shared = {}
    families = {}

    def push(src, dst, device, family, key=None):
        k = shared.get(key)
        if k is None:
            k = count[0]
            count[0] += 1
            if key is not None:
                shared[key] = k
        copy = pltpu.make_async_remote_copy(
            src_ref=src,
            dst_ref=dst,
            send_sem=ssem.at[families.setdefault(family, len(families))],
            recv_sem=rsem.at[k],
            device_id=device,
            device_id_type=MESH,
        )
        copy.start()
        return copy

    def same(ref, device, family, key=None):
        return push(ref, ref, device, family, key)

    def whole(ref, family, key):
        return pltpu.make_async_remote_copy(
            src_ref=ref,
            dst_ref=ref,
            send_sem=ssem.at[families[family]],
            recv_sem=rsem.at[shared[key] if key is not None else 0],
            device_id=twin,
            device_id_type=MESH,
        )

    pl.semaphore_wait(barrier, len(met))

    weights = ((win_ref, w_in), (wout_ref, w_out))
    slices = [[], []]

    def open_ring(a):
        src, w = weights[a]
        for d in range(2):
            push(src.at[:, own_cols], w.at[g, yh, z], ring[d], (0, a), (0, a, d))

    def open_column(a):
        src, w = weights[a]
        for dg, dy in TURNS:
            slices[a].append(
                push(src.at[:, cols_of(dg, dy)], w.at[g, yh, z], column(dg, dy), (0, a))
            )

    def slice_arrives(a, i):
        dg, dy = TURNS[i]
        slices[a][i].wait_recv()
        block = weights[a][1].at[lax.rem(g + dg, 2), lax.rem(yh + dy, 2), z]
        for d in range(2):
            same(block, ring[d], (0, a), (0, a, d))

    ahead = {}

    def ring_arrives(a, s):
        w = weights[a][1]
        for h in range(2):
            for d in range(2):
                if s == 1:
                    if h == 0:
                        whole(w.at[:, :, at(-step_of[d])], (0, a), (0, a, d)).wait_recv()
                elif s < 4 or h == d:
                    ahead[a, s, h, d].wait_recv()
                if s < 3 or (s == 3 and h == d):
                    o = at(-step_of[d] * s)
                    ahead[a, s + 1, h, d] = same(w.at[h, :, o], ring[d], (0, a))

    there = 1 - yh
    arrays = ((tokens_ref, tok), (upstream_ref, up), (corpus_ref, cor))
    from_mate, from_swap, from_side = {}, {}, {}

    def spot(half, h, i, lane):
        return pl.ds(half * groups_of_half + core * 4 + h * 2 + i, 1), lane

    def open_part(k, i):
        src, buf = arrays[k]
        given = src.at[pl.ds(core * 4 + (1 - g) * 2 + i, 1), par]
        from_mate[k, i] = push(given, buf.at[spot(yh, 1 - g, i, par)], mate, (1, k))

    def pass_on(k, i, other):
        block = arrays[k][1].at[spot(there, 1 - g if other else g, i, par)]
        from_side[k, i, other] = same(block, right if i else left, (1, k))
        same(block, twin, (1, k), (1, k))

    def mate_arrives(k, i):
        from_mate[k, i].wait_recv()
        from_swap[k, i] = same(arrays[k][1].at[spot(there, g, i, par)], swap, (1, k))
        pass_on(k, i, 0)

    def swap_arrives(k, i):
        from_swap[k, i].wait_recv()
        pass_on(k, i, 1)

    def side_arrives(k, i, other):
        from_side[k, i, other].wait_recv()
        block = arrays[k][1].at[spot(there, 1 - g if other else g, i, 1 - par)]
        same(block, twin, (1, k), (1, k))

    def after_twin(k):
        start = there * groups_of_half + (1 - core) * 4
        whole(arrays[k][1].at[pl.ds(start, 4)], (1, k), (1, k)).wait_recv()

    def rows_of(x, base, tile, p):
        parts = []
        per = x.shape[1] * x.shape[2]
        for q in range(4):
            at_q = pl.multiple_of(q * NZ * shard + p * 2 * shard, 2 * shard)
            block = x[pl.ds(base, tile // per), :, :, pl.ds(at_q, 2 * shard)]
            parts.append(block.reshape(tile, 2 * shard))
        return jnp.concatenate(parts, axis=1)

    def weight(w, p):
        parts = []
        for q in range(4):
            block = w[q // 2, q % 2, pl.ds(2 * p, 2)]
            parts.append(block.reshape(2 * shard, cut))
        return jnp.concatenate(parts, axis=0)

    def multiply(x, w, acc, half, p, is_first):
        per = x.shape[1] * x.shape[2]
        tile = min(512, per * groups_of_half)
        rows_half = per * groups_of_half

        def body(m, carry):
            base = half * groups_of_half + m * (tile // per)
            rows = pl.ds(pl.multiple_of(half * rows_half + m * tile, tile), tile)
            part_sum = jnp.dot(rows_of(x, base, tile, p), weight(w, p), preferred_element_type=F32)
            acc[rows, :] = part_sum if is_first else acc[rows, :] + part_sum
            return carry

        lax.fori_loop(0, rows_half // tile, body, 0)

    root = math.sqrt(2.0 / math.pi)

    def gelu_parts(p):
        th = jnp.tanh(root * (p + 0.044715 * (p * p * p)))
        return 0.5 * (1.0 + th), th

    slab = 64
    n_tok = acc_p.shape[0]

    def activate():
        def body(m, carry):
            rows = pl.ds(pl.multiple_of(m * slab, slab), slab)
            p = acc_p[rows, :] * scale_in
            cdf, th = gelu_parts(p)
            hid[rows, :] = (p * cdf).astype(BF16)
            acc_p[rows, :] = cdf + (0.5 * root) * p * (1.0 - th * th) * (
                1.0 + (3 * 0.044715) * (p * p)
            )
            return carry

        lax.fori_loop(0, n_tok // slab, body, 0)

    def slope_rows():
        def body(m, carry):
            rows = pl.ds(pl.multiple_of(m * slab, slab), slab)
            dpre[rows, :] = (acc_d[rows, :] * scale_out * acc_p[rows, :]).astype(BF16)
            return carry

        lax.fori_loop(0, n_tok // slab, body, 0)

    open_ring(0)
    open_column(0)
    open_ring(1)
    open_part(0, 0)
    open_column(1)
    open_part(0, 1)
    for k in (1, 2):
        for i in range(2):
            open_part(k, i)
    load_in.wait()
    load_out.wait()
    load_lens.wait()
    load_owners.wait()
    lens_here[...] = per_passage(len_ref, lens_here.shape)
    lens_copy = push(lens_here, lens_there, mate, (2,))
    load_tok.wait()
    load_up.wait()
    events = []

    def event(time, what, *args):
        events.append((time, len(events), what, args))

    for a, at_slice, at_ring in (
        (0, (3.4, 3.5, 3.6), (8.0, 12.5, 17.0, 20.5)),
        (1, (9.0, 9.1, 9.2), (13.5, 18.5)),
    ):
        for i, time in enumerate(at_slice):
            event(time, slice_arrives, a, i)
        for i, time in enumerate(at_ring):
            event(time, ring_arrives, a, i + 1)
            x, w, acc = ((tok, w_in, acc_p), (up, w_out, acc_d))[a]
            event(time + 0.1, multiply, x, w, acc, yh, pairs[i + 1], i == 0)
    hop = 4.5
    for k, times in enumerate(((7.0, 10.5), (13.2, 15.6), (18.7, 19.7))):
        for i, time in enumerate(times):
            event(time, mate_arrives, k, i)
            if k < 2:
                event(time + hop, swap_arrives, k, i)
                event(time + hop + 0.1, side_arrives, k, i, 0)
    for i, time in enumerate((16.0, 19.5)):
        event(time, side_arrives, 0, i, 1)
    event(21.9, side_arrives, 1, 0, 1)
    event(22.0, after_twin, 0)
    for i in range(1, 4):
        event(22.1, multiply, tok, w_in, acc_p, there, pairs[i], i == 1)
    event(22.15, ring_arrives, 1, 3)
    event(22.2, side_arrives, 1, 1, 1)
    event(22.3, multiply, tok, w_in, acc_p, there, pairs[4], False)
    event(22.4, activate)
    for _, _, what, args in sorted(events, key=lambda x: x[:2]):
        what(*args)

    def gradient(x, y, out, scale, p):
        def body(gg, carry):
            parts = []
            for yy in range(2):
                at_q = pl.multiple_of((gg * 2 + yy) * NZ * shard + p * 2 * shard, 2 * shard)
                block = x[:, :, :, pl.ds(at_q, 2 * shard)]
                parts.append(block.reshape(n_tok, 2 * shard))
            both = lax.dot_general(
                jnp.concatenate(parts, axis=1),
                y[...],
                (((0,), (0,)), ((), ())),
                preferred_element_type=F32,
            )
            both = (both * scale).astype(BF16).reshape(2, 2, shard, cut)
            for yy in range(2):
                out[gg, yy, pl.ds(2 * p, 2)] = both[yy]
            return carry

        lax.fori_loop(0, 2, body, 0)

    def add(a, b):
        return (a.astype(F32) + b.astype(F32)).astype(BF16)

    back = {}

    def give_back(a, s):
        grad, arrived = ((g_in, r_in), (g_out, r_out))[a]
        for h in range(2):
            for d in range(2):
                o = at(step_of[d] * (5 - s))
                if s == 1 and h != d:
                    continue
                if s > 2 or (s == 2 and h == d):
                    back[a, s - 1, h, d].wait_recv()
                    for yy in range(2):
                        grad[h, yy, o] = add(grad[h, yy, o], arrived[d, s - 2, h, yy])
                back[a, s, h, d] = push(grad.at[h, :, o], arrived.at[d, s - 1, h], ring[d], (3, a))

    feat = pool.shape[-1]
    rows_c = acc_c.shape[0] // 2
    mine = pl.ds(pl.multiple_of(t * feat, feat), feat)

    def pool_rows():
        after_twin(2)
        lens_copy.wait_recv()
        load_cor.wait()
        for half in (yh, there):
            for k in range(1, 5):
                multiply(cor, w_in, acc_c, half, pairs[k], k == 1)
        shape = (passages, rows_c)
        row = lax.broadcasted_iota(jnp.int32, shape, 0)
        col = lax.broadcasted_iota(jnp.int32, shape, 1)
        stack = []
        for half, lens in ((yh, lens_here), (there, lens_there)):
            span = pl.ds(pl.multiple_of(half * rows_c, rows_c), rows_c)
            pre = acc_c[span, :] * scale_in
            cdf, _ = gelu_parts(pre)
            ch = (pre * cdf).astype(BF16)
            stop = row * plen + jnp.broadcast_to(lens[:, :1], shape)
            inside = jnp.logical_and(col >= row * plen, col < stop)
            live = jnp.where(inside, 1.0, 0.0).astype(BF16)
            if not stack:
                x = cor[pl.ds(yh * groups_of_half, groups_of_half), :, :, mine]
                base = jnp.dot(live, x.reshape(rows_c, feat), preferred_element_type=F32)
            ph = jnp.dot(live, ch, preferred_element_type=F32)
            hi = ph.astype(BF16).astype(F32)
            stack += [hi, ph - hi]
        hl = jnp.concatenate(stack, axis=0).astype(BF16)

        def branch(q, carry):
            w = w_out[q // 2, lax.rem(q, 2)].reshape(NZ * shard, cut)
            both = lax.dot_general(hl, w, (((1,), (1,)), ((), ())), preferred_element_type=F32)
            both = both * scale_out
            n = NZ * shard // feat
            for i in range(2):
                rows = both[2 * i * passages : (2 * i + 1) * passages]
                rows = rows + both[(2 * i + 1) * passages : (2 * i + 2) * passages]
                for k in range(n):
                    pool[i, q * n + k] = rows[:, k * feat : (k + 1) * feat]
            return carry

        lax.fori_loop(0, 4, branch, 0)
        for dy in range(2):
            for dg in range(2):
                for dt in range(NT):
                    if dy or dg or dt:
                        src = pool.at[dy, lax.rem(t + dt, NT)]
                        slot = pool_in.at[(dy * 2 + dg) * NT + dt]
                        push(src, slot, cell(dg, dy, dt), (4,), (4,))
        return (base,)

    def square_rows(base):
        total = base + pool[0, t]
        whole(pool_in.at[pl.ds(1, 4 * NT - 1)], (4,), (4,)).wait_recv()
        for k in range(1, 4 * NT):
            total = total + pool_in[k]
        lens = jnp.broadcast_to(lens_here[:, :1], total.shape)
        pooled = total * (1.0 / lens.astype(F32))
        own_square = jnp.sum(pooled * pooled, axis=1, keepdims=True)
        square[...] = jnp.broadcast_to(own_square, square.shape)
        for dt in range(1, NT):
            push(square, square_in.at[dt], cell(0, 0, dt), (5,), (5,))
        return pooled, own_square

    def post_rows(pooled, own_square):
        whole(square_in.at[pl.ds(1, NT - 1)], (5,), (5,)).wait_recv()
        total = own_square
        for dt in range(1, NT):
            total = total + square_in[dt][:, :1]
        rows = pooled * lax.rsqrt(total / (NT * feat) + EPSILON)
        owners = per_passage(owner_ref, rows.shape)
        for a in range(2):
            for b in range(NZ):
                to_yh, to_z = lax.rem(yh + a, 2), at(b)
                owner = (g * 2 + to_yh) * NZ + to_z
                row = jnp.sum(jnp.where(owners == owner, rows, 0.0), axis=0, keepdims=True)
                if a or b:
                    letter[a * NZ + b] = row
                    push(
                        letter.at[a * NZ + b],
                        letter_in.at[yh * NZ + z],
                        (g, to_yh, to_z, t),
                        (6,),
                        (6,),
                    )
                else:
                    letter_in[yh * NZ + z] = row

    def read_rows():
        whole(letter_in.at[pl.ds(0, 2 * NZ - 1)], (6,), (6,)).wait_recv()
        row = lax.broadcasted_iota(jnp.int32, index_ref.shape, 0)
        out = jnp.zeros(index_ref.shape, F32)
        for d in range(2 * NZ):
            out = jnp.where(row == d, jnp.broadcast_to(letter_in[d], out.shape), out)
        index_ref[...] = out.astype(BF16)

    outs = (new_in_ref, new_out_ref)
    sums = ((g_in, r_in, w_in), (g_out, r_out, w_out))

    def settle(a):
        grad, arrived, w = sums[a]
        for h in range(2):
            for d in range(2):
                back[a, 4, h, d].wait_recv()
        for i, (dg, dy) in enumerate(TURNS + ((0, 0),)):
            gg, yy = lax.rem(g + dg, 2), lax.rem(yh + dy, 2)
            total = (
                grad[gg, yy, z].astype(F32)
                + arrived[0, 3, gg, yy].astype(F32)
                + arrived[1, 3, gg, yy].astype(F32)
            )
            fin[a, i] = (w[gg, yy, z].astype(F32) - LEARN_RATE * total).astype(BF16)
            target = outs[a].at[:, own_cols]
            if dg or dy:
                push(fin.at[a, i], target, column(dg, dy), (7, a), (7, a))
            else:
                load(fin.at[a, i], target)

    def grad_out(j):
        gradient(up, hid, g_out, scale_out, pairs[j])

    def grad_in(j):
        gradient(tok, dpre, g_in, scale_in, pairs[j])

    after_twin(1)
    grad_out(4)
    give_back(1, 1)
    for i in range(2):
        swap_arrives(2, i)
        side_arrives(2, i, 0)
    grad_out(3)
    multiply(up, w_out, acc_d, yh, pairs[3], False)
    for k in range(1, 4):
        multiply(up, w_out, acc_d, there, pairs[k], k == 1)
    give_back(1, 2)
    ring_arrives(1, 4)
    for half in (yh, there):
        multiply(up, w_out, acc_d, half, pairs[4], False)
    slope_rows()
    grad_in(4)
    give_back(0, 1)
    for i in range(2):
        side_arrives(2, i, 1)
    grad_out(2)
    stage = pool_rows()
    give_back(1, 3)
    grad_in(3)
    give_back(0, 2)
    grad_out(1)
    give_back(1, 4)
    grad_in(2)
    give_back(0, 3)
    stage = square_rows(*stage)
    grad_in(1)
    give_back(0, 4)
    stage = post_rows(*stage)
    settle(1)
    settle(0)
    read_rows()
    for a in range(2):
        whole(outs[a].at[:, pl.ds(0, 3 * cut)], (7, a), (7, a)).wait_recv()
    for copy in loads[7:]:
        copy.wait()
    covers = [((0, 0), acc_p.at[pl.ds(0, 31 * n_tok // 32)])]
    covers += [((0, 1), acc_d.at[pl.ds(0, 31 * n_tok // 32)])]
    covers += [((1, k), arrays[k][1].at[pl.ds(0, groups_of_half)]) for k in range(3)]
    covers += [((2,), lens_here), ((4,), pool_in.at[pl.ds(1, 4 * NT - 1)])]
    covers += [((3, a), sums[a][0].at[:, :, pl.ds(0, NZ - 1)]) for a in range(2)]
    covers += [((5,), square_in.at[pl.ds(1, NT - 1)]), ((6,), letter_in.at[pl.ds(0, 2 * NZ - 1)])]
    covers += [((7, a), fin.at[a, pl.ds(0, 3)]) for a in range(2)]
    for family, ref in covers:
        whole(ref, family, None).wait_send()


def pass_through(*refs):
    n = len(refs) // 3
    sources, results, held = refs[:n], refs[n : 2 * n], refs[2 * n : 3 * n]
    sems = refs[3 * n]
    taken = []
    for k in range(n):
        copy = pltpu.make_async_copy(sources[k], held[k], sems.at[k])
        copy.start()
        taken.append(copy)
    given = []
    for k in range(n):
        taken[k].wait()
        copy = pltpu.make_async_copy(held[k], results[k], sems.at[n + k])
        copy.start()
        given.append(copy)
    for copy in given:
        copy.wait()


def handed_over(*arrays):
    any_spec = pl.BlockSpec(memory_space=pl.ANY)
    return pl.pallas_call(
        pass_through,
        out_shape=tuple(jax.ShapeDtypeStruct(x.shape, x.dtype) for x in arrays),
        in_specs=[any_spec] * len(arrays),
        out_specs=(any_spec,) * len(arrays),
        scratch_shapes=[pltpu.VMEM(x.shape, x.dtype) for x in arrays]
        + [pltpu.SemaphoreType.DMA((2 * len(arrays),))],
    )(*arrays)


def fused(tokens, upstream, corpus, lengths, owners, w_in, w_out, scale_in, scale_out):
    shard, local_ff = w_in.shape
    cut = local_ff // 4
    n_tok, width = tokens.shape
    n_corpus = corpus.shape[0]
    npass = lengths.shape[0]
    full = (2, 2, NZ, shard, cut)
    n_sem = N_SEM
    feat = width // NT
    rows_t, rows_c = n_tok // 16, n_corpus // 16
    any_spec = pl.BlockSpec(memory_space=pl.ANY)
    vmem_spec = pl.BlockSpec(memory_space=pltpu.VMEM)
    return pl.pallas_call(
        functools.partial(kernel, n_corpus // npass, scale_in, scale_out),
        out_shape=(
            jax.ShapeDtypeStruct((shard, local_ff), BF16),
            jax.ShapeDtypeStruct((shard, local_ff), BF16),
            jax.ShapeDtypeStruct((2 * NZ, feat), BF16),
        ),
        in_specs=[any_spec] * 7,
        out_specs=(any_spec, any_spec, vmem_spec),
        scratch_shapes=[
            pltpu.VMEM((16, 2, rows_t, width), BF16),
            pltpu.VMEM((16, 2, rows_t, width), BF16),
            pltpu.VMEM((16, 2, rows_c, width), BF16),
            pltpu.VMEM(full, BF16),
            pltpu.VMEM(full, BF16),
            pltpu.VMEM((2 * n_tok, cut), F32),
            pltpu.VMEM((2 * n_tok, cut), F32),
            pltpu.VMEM((2 * n_corpus, cut), F32),
            pltpu.VMEM((2 * n_tok, cut), BF16),
            pltpu.VMEM((2 * n_tok, cut), BF16),
            pltpu.VMEM(full, BF16),
            pltpu.VMEM(full, BF16),
            pltpu.VMEM((2, 4, 2, 2, shard, cut), BF16),
            pltpu.VMEM((2, 4, 2, 2, shard, cut), BF16),
            pltpu.VMEM((2, 4, shard, cut), BF16),
            pltpu.VMEM((npass, 128), jnp.int32),
            pltpu.VMEM((npass, 128), jnp.int32),
            pltpu.VMEM((2, NT, npass, feat), F32),
            pltpu.VMEM((4 * NT, npass, feat), F32),
            pltpu.VMEM((npass, 128), F32),
            pltpu.VMEM((NT, npass, 128), F32),
            pltpu.VMEM((2 * NZ, 1, feat), F32),
            pltpu.VMEM((2 * NZ, 1, feat), F32),
            pltpu.SMEM((npass,), jnp.int32),
            pltpu.SMEM((npass,), jnp.int32),
            pltpu.SemaphoreType.DMA((9,)),
            pltpu.SemaphoreType.DMA((13,)),
            pltpu.SemaphoreType.DMA((n_sem,)),
        ],
        compiler_params=pltpu.CompilerParams(
            collective_id=0, has_side_effects=True, vmem_limit_bytes=60 * 1024 * 1024
        ),
    )(
        tokens.reshape(8, 2, rows_t, width),
        upstream.reshape(8, 2, rows_t, width),
        corpus.reshape(8, 2, rows_c, width),
        lengths,
        owners,
        w_in,
        w_out,
    )


def local(tokens, upstream, corpus, lengths, owners, w_in, w_out):
    width = w_in.shape[0] * lax.axis_size(GROUP_DP)
    hidden_units = w_in.shape[1] * lax.axis_size("tensor")
    scale_in = 1.0 / math.sqrt(width)
    scale_out = 1.0 / math.sqrt(hidden_units)
    return handed_over(
        *fused(tokens, upstream, corpus, lengths, owners, w_in, w_out, scale_in, scale_out)
    )


def solution(mesh):
    torus = Mesh(
        mesh.devices.reshape(mesh.shape["group"], 2, NZ, mesh.shape["tensor"]),
        ("group", "dp_0", "dp_1", "tensor"),
    )
    return jax.shard_map(
        local,
        mesh=torus,
        in_specs=(
            P(DP, None),
            P(DP, None),
            P(DP, None),
            P(DP),
            P(DP),
            P(GROUP_DP, "tensor"),
            P(GROUP_DP, "tensor"),
        ),
        out_specs=(P(GROUP_DP, "tensor"), P(GROUP_DP, "tensor"), P(GROUP_DP, "tensor")),
        check_vma=False,
    )
```

time: 83 us -> 73.1 us (0.88)
  Pallas kernels: 77.7 us -> 72.2 us
  local copies, waits for them, and re-layouts: 4.43 us -> 0 us
    pallas_call x1, Pallas kernels: 77.7 us -> 70.5 us  [fused(): pl.pallas_call(functools.partial(kernel, n_corpus // npass, scale_in, sca...]
    unnamed x3 -> x0, local copies, waits for them, and re-layouts: 4.43 us -> none
    pallas_call x0 -> x1, Pallas kernels: none -> 1.68 us  [handed_over(): pl.pallas_call(pass_through, out_shape=tuple((jax.ShapeDtypeStruct(x.shap...]
where the time goes in v4:
time: 73.1 us; the launch traced here: 72.9 us
  Pallas kernels  72.2 us (99%)
    pallas_call x1, Pallas kernels, fused(): pl.pallas_call(functools.partial(kernel, n_corpus // npass, scale_in, sca...  70.5 us
    pallas_call x1, Pallas kernels, handed_over(): pl.pallas_call(pass_through, out_shape=tuple((jax.ShapeDtypeStruct(x.shap...  1.68 us

profile of v4, /device:TPU:1, one launch (start us, length us, event | category | flops | bytes accessed | tf_op | source)
XLA Modules:
  0.0 72.9 jit_solution(11328022836251076665)
XLA Ops:
  0.6 70.5 %shard_map.94 = (bf16[64,1024]{1,0:T(8,128)(2,1)}, bf16[64,1024]{1,0:T(8,128)(2,1)}, bf16[16,256]{1,0:T(8,128)(2,1)}) custom-call(bf16[8,2,32,2048]{3,2,1,0:T(8,128)(2,1)} %bitcast.3, bf16[8,2,32,2048]{3,2,1,0:T(8,128)(2,1)} %bitcast.4, bf16[8,2,16,2048]{3,2,1,0:T(8,128)(2,1)} %bitcast.5, s32[8]{0:T(128)} %len_hbm.1, s32[8]{0:T(128)} %owner_hbm.1, ...), custom_call_target="tpu_custom_call" | custom-call | tf_op jit(solution)/shard_map/pallas_call | solution.py:624
  71.2 1.7 %shard_map.95 = (bf16[64,1024]{1,0:T(8,128)(2,1)}, bf16[64,1024]{1,0:T(8,128)(2,1)}, bf16[16,256]{1,0:T(8,128)(2,1)}) custom-call(bf16[64,1024]{1,0:T(8,128)(2,1)} %get-tuple-element.6.refs_0_, bf16[64,1024]{1,0:T(8,128)(2,1)} %get-tuple-element.7.refs_1_, bf16[16,256]{1,0:T(8,128)(2,1)} %get-tuple-element.8.refs_2_), custom_call_target="tpu_custom_call" | custom-call | tf_op jit(solution)/shard_map/pallas_call | solution.py:602

commit v5 on v4

--- a/solution.py
+++ b/solution.py
@@ -19,7 +19,7 @@
 BF16 = jnp.bfloat16
 NZ = 8
 NT = 8
-N_SEM = 91
+N_SEM = 107
 TURNS = ((1, 1), (1, 0), (0, 1))
 
 
@@ -221,31 +221,34 @@
     arrays = ((tokens_ref, tok), (upstream_ref, up), (corpus_ref, cor))
     from_mate, from_swap, from_side = {}, {}, {}
 
-    def spot(half, h, i, lane):
-        return pl.ds(half * groups_of_half + core * 4 + h * 2 + i, 1), lane
-
-    def open_part(k, i):
+    fine = 16
+
+    def spot(half, h, i, lane, r):
+        start = half * groups_of_half + core * 4 + h * 2 + i
+        return pl.ds(start, 1), lane, pl.ds(r * fine, fine)
+
+    def open_part(k, i, r):
         src, buf = arrays[k]
-        given = src.at[pl.ds(core * 4 + (1 - g) * 2 + i, 1), par]
-        from_mate[k, i] = push(given, buf.at[spot(yh, 1 - g, i, par)], mate, (1, k))
-
-    def pass_on(k, i, other):
-        block = arrays[k][1].at[spot(there, 1 - g if other else g, i, par)]
-        from_side[k, i, other] = same(block, right if i else left, (1, k))
+        given = src.at[pl.ds(core * 4 + (1 - g) * 2 + i, 1), par, pl.ds(r * fine, fine)]
+        from_mate[k, i, r] = push(given, buf.at[spot(yh, 1 - g, i, par, r)], mate, (1, k))
+
+    def pass_on(k, i, r, other):
+        block = arrays[k][1].at[spot(there, 1 - g if other else g, i, par, r)]
+        from_side[k, i, r, other] = same(block, right if i else left, (1, k))
         same(block, twin, (1, k), (1, k))
 
-    def mate_arrives(k, i):
-        from_mate[k, i].wait_recv()
-        from_swap[k, i] = same(arrays[k][1].at[spot(there, g, i, par)], swap, (1, k))
-        pass_on(k, i, 0)
-
-    def swap_arrives(k, i):
-        from_swap[k, i].wait_recv()
-        pass_on(k, i, 1)
-
-    def side_arrives(k, i, other):
-        from_side[k, i, other].wait_recv()
-        block = arrays[k][1].at[spot(there, 1 - g if other else g, i, 1 - par)]
+    def mate_arrives(k, i, r):
+        from_mate[k, i, r].wait_recv()
+        from_swap[k, i, r] = same(arrays[k][1].at[spot(there, g, i, par, r)], swap, (1, k))
+        pass_on(k, i, r, 0)
+
+    def swap_arrives(k, i, r):
+        from_swap[k, i, r].wait_recv()
+        pass_on(k, i, r, 1)
+
+    def side_arrives(k, i, r, other):
+        from_side[k, i, r, other].wait_recv()
+        block = arrays[k][1].at[spot(there, 1 - g if other else g, i, 1 - par, r)]
         same(block, twin, (1, k), (1, k))
 
     def after_twin(k):
@@ -312,15 +315,19 @@
 
         lax.fori_loop(0, n_tok // slab, body, 0)
 
+    order = ((0, 0), (1, 0), (0, 1), (1, 1))
     open_ring(0)
     open_column(0)
     open_ring(1)
-    open_part(0, 0)
+    for i, r in order[:2]:
+        open_part(0, i, r)
     open_column(1)
-    open_part(0, 1)
-    for k in (1, 2):
-        for i in range(2):
-            open_part(k, i)
+    for i, r in order[2:]:
+        open_part(0, i, r)
+    for i, r in order:
+        open_part(1, i, r)
+    for i in range(2):
+        open_part(2, i, 0)
     load_in.wait()
     load_out.wait()
     load_lens.wait()
@@ -329,6 +336,7 @@
     lens_copy = push(lens_here, lens_there, mate, (2,))
     load_tok.wait()
     load_up.wait()
+    load_cor.wait()
     events = []
 
     def event(time, what, *args):
@@ -336,7 +344,7 @@
 
     for a, at_slice, at_ring in (
         (0, (3.4, 3.5, 3.6), (8.0, 12.5, 17.0, 20.5)),
-        (1, (9.0, 9.1, 9.2), (13.5, 18.5)),
+        (1, (7.5, 7.6, 7.7), (13.5, 18.0, 21.8)),
     ):
         for i, time in enumerate(at_slice):
             event(time, slice_arrives, a, i)
@@ -344,23 +352,25 @@
             event(time, ring_arrives, a, i + 1)
             x, w, acc = ((tok, w_in, acc_p), (up, w_out, acc_d))[a]
             event(time + 0.1, multiply, x, w, acc, yh, pairs[i + 1], i == 0)
-    hop = 4.5
-    for k, times in enumerate(((7.0, 10.5), (13.2, 15.6), (18.7, 19.7))):
-        for i, time in enumerate(times):
-            event(time, mate_arrives, k, i)
-            if k < 2:
-                event(time + hop, swap_arrives, k, i)
-                event(time + hop + 0.1, side_arrives, k, i, 0)
-    for i, time in enumerate((16.0, 19.5)):
-        event(time, side_arrives, 0, i, 1)
-    event(21.9, side_arrives, 1, 0, 1)
-    event(22.0, after_twin, 0)
+            if a == 0 and i < 3:
+                event(time + 0.2, multiply, cor, w_in, acc_c, yh, pairs[i + 1], i == 0)
+    hop = 3.3
+    for k, times in enumerate(((5.8, 7.2, 9.2, 10.6), (12.0, 13.4, 14.8, 16.2))):
+        for (i, r), time in zip(order, times):
+            event(time, mate_arrives, k, i, r)
+            event(time + hop, swap_arrives, k, i, r)
+            event(time + hop + 0.1, side_arrives, k, i, r, 0)
+            event(time + 2 * hop + 0.2, side_arrives, k, i, r, 1)
+    for i, time in enumerate((18.0, 19.4)):
+        event(time, mate_arrives, 2, i, 0)
+    event(19.6, after_twin, 0)
     for i in range(1, 4):
-        event(22.1, multiply, tok, w_in, acc_p, there, pairs[i], i == 1)
-    event(22.15, ring_arrives, 1, 3)
-    event(22.2, side_arrives, 1, 1, 1)
-    event(22.3, multiply, tok, w_in, acc_p, there, pairs[4], False)
-    event(22.4, activate)
+        event(19.7, multiply, tok, w_in, acc_p, there, pairs[i], i == 1)
+    event(20.7, multiply, tok, w_in, acc_p, there, pairs[4], False)
+    for i in range(2):
+        event(20.8, swap_arrives, 2, i, 0)
+        event(20.8, side_arrives, 2, i, 0, 0)
+    event(20.9, activate)
     for _, _, what, args in sorted(events, key=lambda x: x[:2]):
         what(*args)
 
@@ -404,15 +414,14 @@
 
     feat = pool.shape[-1]
     rows_c = acc_c.shape[0] // 2
-    mine = pl.ds(pl.multiple_of(t * feat, feat), feat)
+    mine = pl.ds(pl.multiple_of((2 * t + g) * feat, feat), feat)
 
     def pool_rows():
         after_twin(2)
         lens_copy.wait_recv()
-        load_cor.wait()
-        for half in (yh, there):
-            for k in range(1, 5):
-                multiply(cor, w_in, acc_c, half, pairs[k], k == 1)
+        multiply(cor, w_in, acc_c, yh, pairs[4], False)
+        for k in range(1, 5):
+            multiply(cor, w_in, acc_c, there, pairs[k], k == 1)
         shape = (passages, rows_c)
         row = lax.broadcasted_iota(jnp.int32, shape, 0)
         col = lax.broadcasted_iota(jnp.int32, shape, 1)
@@ -450,13 +459,14 @@
             for dg in range(2):
                 for dt in range(NT):
                     if dy or dg or dt:
-                        src = pool.at[dy, lax.rem(t + dt, NT)]
+                        to_g, _, _, to_t = cell(dg, dy, dt)
+                        src = pool.at[dy, 2 * to_t + to_g]
                         slot = pool_in.at[(dy * 2 + dg) * NT + dt]
                         push(src, slot, cell(dg, dy, dt), (4,), (4,))
         return (base,)
 
     def square_rows(base):
-        total = base + pool[0, t]
+        total = base + pool[0, 2 * t + g]
         whole(pool_in.at[pl.ds(1, 4 * NT - 1)], (4,), (4,)).wait_recv()
         for k in range(1, 4 * NT):
             total = total + pool_in[k]
@@ -464,41 +474,40 @@
         pooled = total * (1.0 / lens.astype(F32))
         own_square = jnp.sum(pooled * pooled, axis=1, keepdims=True)
         square[...] = jnp.broadcast_to(own_square, square.shape)
-        for dt in range(1, NT):
-            push(square, square_in.at[dt], cell(0, 0, dt), (5,), (5,))
+        for k in range(1, 2 * NT):
+            push(square, square_in.at[k], cell(k // NT, 0, k % NT), (5,), (5,))
         return pooled, own_square
 
     def post_rows(pooled, own_square):
-        whole(square_in.at[pl.ds(1, NT - 1)], (5,), (5,)).wait_recv()
+        whole(square_in.at[pl.ds(1, 2 * NT - 1)], (5,), (5,)).wait_recv()
         total = own_square
-        for dt in range(1, NT):
-            total = total + square_in[dt][:, :1]
-        rows = pooled * lax.rsqrt(total / (NT * feat) + EPSILON)
+        for k in range(1, 2 * NT):
+            total = total + square_in[k][:, :1]
+        rows = pooled * lax.rsqrt(total / (2 * NT * feat) + EPSILON)
         owners = per_passage(owner_ref, rows.shape)
-        for a in range(2):
-            for b in range(NZ):
-                to_yh, to_z = lax.rem(yh + a, 2), at(b)
-                owner = (g * 2 + to_yh) * NZ + to_z
-                row = jnp.sum(jnp.where(owners == owner, rows, 0.0), axis=0, keepdims=True)
-                if a or b:
-                    letter[a * NZ + b] = row
-                    push(
-                        letter.at[a * NZ + b],
-                        letter_in.at[yh * NZ + z],
-                        (g, to_yh, to_z, t),
-                        (6,),
-                        (6,),
-                    )
-                else:
-                    letter_in[yh * NZ + z] = row
+        here_slot = (g * 2 + yh) * NZ + z
+        for k in range(4 * NZ):
+            to_g, to_yh = lax.rem(g + k // (2 * NZ), 2), lax.rem(yh + k // NZ, 2)
+            to_z = at(k % NZ)
+            owner = (to_g * 2 + to_yh) * NZ + to_z
+            row = jnp.sum(jnp.where(owners == owner, rows, 0.0), axis=0, keepdims=True)
+            if k:
+                letter[k] = row
+                push(
+                    letter.at[k], letter_in.at[here_slot], (to_g, to_yh, to_z, t), (6,), (6,)
+                )
+            else:
+                letter_in[here_slot] = row
 
     def read_rows():
-        whole(letter_in.at[pl.ds(0, 2 * NZ - 1)], (6,), (6,)).wait_recv()
-        row = lax.broadcasted_iota(jnp.int32, index_ref.shape, 0)
-        out = jnp.zeros(index_ref.shape, F32)
-        for d in range(2 * NZ):
-            out = jnp.where(row == d, jnp.broadcast_to(letter_in[d], out.shape), out)
-        index_ref[...] = out.astype(BF16)
+        whole(letter_in.at[pl.ds(0, 4 * NZ - 1)], (6,), (6,)).wait_recv()
+        shape = (2 * NZ, feat)
+        row = lax.broadcasted_iota(jnp.int32, shape, 0)
+        for gg in range(2):
+            out = jnp.zeros(shape, F32)
+            for d in range(2 * NZ):
+                out = jnp.where(row == d, jnp.broadcast_to(letter_in[gg * 2 * NZ + d], shape), out)
+            index_ref[:, gg * feat : (gg + 1) * feat] = out.astype(BF16)
 
     outs = (new_in_ref, new_out_ref)
     sums = ((g_in, r_in, w_in), (g_out, r_out, w_out))
@@ -531,35 +540,30 @@
     after_twin(1)
     grad_out(4)
     give_back(1, 1)
+    ring_arrives(1, 4)
+    multiply(up, w_out, acc_d, yh, pairs[4], False)
+    for k in range(1, 5):
+        multiply(up, w_out, acc_d, there, pairs[k], k == 1)
+    slope_rows()
     for i in range(2):
-        swap_arrives(2, i)
-        side_arrives(2, i, 0)
-    grad_out(3)
-    multiply(up, w_out, acc_d, yh, pairs[3], False)
-    for k in range(1, 4):
-        multiply(up, w_out, acc_d, there, pairs[k], k == 1)
-    give_back(1, 2)
-    ring_arrives(1, 4)
-    for half in (yh, there):
-        multiply(up, w_out, acc_d, half, pairs[4], False)
-    slope_rows()
+        side_arrives(2, i, 0, 1)
     grad_in(4)
     give_back(0, 1)
-    for i in range(2):
-        side_arrives(2, i, 1)
-    grad_out(2)
+    grad_out(3)
+    give_back(1, 2)
     stage = pool_rows()
-    give_back(1, 3)
     grad_in(3)
     give_back(0, 2)
-    grad_out(1)
-    give_back(1, 4)
+    grad_out(2)
+    give_back(1, 3)
     grad_in(2)
     give_back(0, 3)
     stage = square_rows(*stage)
+    grad_out(1)
+    give_back(1, 4)
     grad_in(1)
     give_back(0, 4)
-    stage = post_rows(*stage)
+    post_rows(*stage)
     settle(1)
     settle(0)
     read_rows()
@@ -572,7 +576,7 @@
     covers += [((1, k), arrays[k][1].at[pl.ds(0, groups_of_half)]) for k in range(3)]
     covers += [((2,), lens_here), ((4,), pool_in.at[pl.ds(1, 4 * NT - 1)])]
     covers += [((3, a), sums[a][0].at[:, :, pl.ds(0, NZ - 1)]) for a in range(2)]
-    covers += [((5,), square_in.at[pl.ds(1, NT - 1)]), ((6,), letter_in.at[pl.ds(0, 2 * NZ - 1)])]
+    covers += [((5,), square_in.at[pl.ds(1, 2 * NT - 1)]), ((6,), letter_in.at[pl.ds(0, 4 * NZ - 1)])]
     covers += [((7, a), fin.at[a, pl.ds(0, 3)]) for a in range(2)]
     for family, ref in covers:
         whole(ref, family, None).wait_send()
@@ -617,7 +621,7 @@
     npass = lengths.shape[0]
     full = (2, 2, NZ, shard, cut)
     n_sem = N_SEM
-    feat = width // NT
+    feat = width // (2 * NT)
     rows_t, rows_c = n_tok // 16, n_corpus // 16
     any_spec = pl.BlockSpec(memory_space=pl.ANY)
     vmem_spec = pl.BlockSpec(memory_space=pltpu.VMEM)
@@ -626,7 +630,7 @@
         out_shape=(
             jax.ShapeDtypeStruct((shard, local_ff), BF16),
             jax.ShapeDtypeStruct((shard, local_ff), BF16),
-            jax.ShapeDtypeStruct((2 * NZ, feat), BF16),
+            jax.ShapeDtypeStruct((2 * NZ, 2 * feat), BF16),
         ),
         in_specs=[any_spec] * 7,
         out_specs=(any_spec, any_spec, vmem_spec),
@@ -648,12 +652,12 @@
             pltpu.VMEM((2, 4, shard, cut), BF16),
             pltpu.VMEM((npass, 128), jnp.int32),
             pltpu.VMEM((npass, 128), jnp.int32),
-            pltpu.VMEM((2, NT, npass, feat), F32),
+            pltpu.VMEM((2, 2 * NT, npass, feat), F32),
             pltpu.VMEM((4 * NT, npass, feat), F32),
             pltpu.VMEM((npass, 128), F32),
-            pltpu.VMEM((NT, npass, 128), F32),
-            pltpu.VMEM((2 * NZ, 1, feat), F32),
-            pltpu.VMEM((2 * NZ, 1, feat), F32),
+            pltpu.VMEM((2 * NT, npass, 128), F32),
+            pltpu.VMEM((4 * NZ, 1, feat), F32),
+            pltpu.VMEM((4 * NZ, 1, feat), F32),
             pltpu.SMEM((npass,), jnp.int32),
             pltpu.SMEM((npass,), jnp.int32),
             pltpu.SemaphoreType.DMA((9,)),

time: 73.1 us -> 71.2 us (0.974)
  Pallas kernels: 72.2 us -> 70.5 us
    pallas_call x1, Pallas kernels: 70.5 us -> 68.8 us  [fused(): pl.pallas_call(functools.partial(kernel, n_corpus // npass, scale_in, sca...]
where the time goes in v5:
time: 71.2 us; the launch traced here: 71.1 us
  Pallas kernels  70.5 us (99%)
    pallas_call x1, Pallas kernels, fused(): pl.pallas_call(functools.partial(kernel, n_corpus // npass, scale_in, sca...  68.8 us
    pallas_call x1, Pallas kernels, handed_over(): pl.pallas_call(pass_through, out_shape=tuple((jax.ShapeDtypeStruct(x.shap...  1.68 us

profile of v5, /device:TPU:1, one launch (start us, length us, event | category | flops | bytes accessed | tf_op | source)
XLA Modules:
  0.0 71.1 jit_solution(13378852662129701779)
XLA Ops:
  0.6 68.8 %shard_map.94 = (bf16[64,1024]{1,0:T(8,128)(2,1)}, bf16[64,1024]{1,0:T(8,128)(2,1)}, bf16[16,256]{1,0:T(8,128)(2,1)}) custom-call(bf16[8,2,32,2048]{3,2,1,0:T(8,128)(2,1)} %bitcast.3, bf16[8,2,32,2048]{3,2,1,0:T(8,128)(2,1)} %bitcast.4, bf16[8,2,16,2048]{3,2,1,0:T(8,128)(2,1)} %bitcast.5, s32[8]{0:T(128)} %len_hbm.1, s32[8]{0:T(128)} %owner_hbm.1, ...), custom_call_target="tpu_custom_call" | custom-call | tf_op jit(solution)/shard_map/pallas_call | solution.py:628
  69.4 1.7 %shard_map.95 = (bf16[64,1024]{1,0:T(8,128)(2,1)}, bf16[64,1024]{1,0:T(8,128)(2,1)}, bf16[16,256]{1,0:T(8,128)(2,1)}) custom-call(bf16[64,1024]{1,0:T(8,128)(2,1)} %get-tuple-element.6.refs_0_, bf16[64,1024]{1,0:T(8,128)(2,1)} %get-tuple-element.7.refs_1_, bf16[16,256]{1,0:T(8,128)(2,1)} %get-tuple-element.8.refs_2_), custom_call_target="tpu_custom_call" | custom-call | tf_op jit(solution)/shard_map/pallas_call | solution.py:606

commit v6 on v5

--- a/solution.py
+++ b/solution.py
@@ -52,6 +52,7 @@
     r_in,
     r_out,
     fin,
+    held,
     lens_here,
     lens_there,
     pool,
@@ -116,6 +117,7 @@
 
     load_lens = load(len_hbm, len_ref)
     load_owners = load(owner_hbm, owner_ref)
+    load_rows = [load(win_ref, held.at[0]), load(wout_ref, held.at[1])]
     load_in = load(win_ref.at[:, own_cols], w_in.at[g, yh, z])
     load_out = load(wout_ref.at[:, own_cols], w_out.at[g, yh, z])
     load_tok = load(tokens_ref, tok.at[here])
@@ -180,7 +182,7 @@
 
     pl.semaphore_wait(barrier, len(met))
 
-    weights = ((win_ref, w_in), (wout_ref, w_out))
+    weights = ((held.at[0], w_in), (held.at[1], w_out))
     slices = [[], []]
 
     def open_ring(a):
@@ -228,9 +230,8 @@
         return pl.ds(start, 1), lane, pl.ds(r * fine, fine)
 
     def open_part(k, i, r):
-        src, buf = arrays[k]
-        given = src.at[pl.ds(core * 4 + (1 - g) * 2 + i, 1), par, pl.ds(r * fine, fine)]
-        from_mate[k, i, r] = push(given, buf.at[spot(yh, 1 - g, i, par, r)], mate, (1, k))
+        buf = arrays[k][1]
+        from_mate[k, i, r] = same(buf.at[spot(yh, 1 - g, i, par, r)], mate, (1, k))
 
     def pass_on(k, i, r, other):
         block = arrays[k][1].at[spot(there, 1 - g if other else g, i, par, r)]
@@ -316,16 +317,21 @@
         lax.fori_loop(0, n_tok // slab, body, 0)
 
     order = ((0, 0), (1, 0), (0, 1), (1, 1))
+    for copy in load_rows:
+        copy.wait()
     open_ring(0)
     open_column(0)
     open_ring(1)
+    load_tok.wait()
     for i, r in order[:2]:
         open_part(0, i, r)
     open_column(1)
     for i, r in order[2:]:
         open_part(0, i, r)
+    load_up.wait()
     for i, r in order:
         open_part(1, i, r)
+    load_cor.wait()
     for i in range(2):
         open_part(2, i, 0)
     load_in.wait()
@@ -334,17 +340,14 @@
     load_owners.wait()
     lens_here[...] = per_passage(len_ref, lens_here.shape)
     lens_copy = push(lens_here, lens_there, mate, (2,))
-    load_tok.wait()
-    load_up.wait()
-    load_cor.wait()
     events = []
 
     def event(time, what, *args):
         events.append((time, len(events), what, args))
 
     for a, at_slice, at_ring in (
-        (0, (3.4, 3.5, 3.6), (8.0, 12.5, 17.0, 20.5)),
-        (1, (7.5, 7.6, 7.7), (13.5, 18.0, 21.8)),
+        (0, (3.4, 3.5, 3.6), (8.0, 13.7, 18.0, 21.5)),
+        (1, (7.5, 7.6, 7.7), (14.5, 19.5, 23.0)),
     ):
         for i, time in enumerate(at_slice):
             event(time, slice_arrives, a, i)
@@ -354,23 +357,22 @@
             event(time + 0.1, multiply, x, w, acc, yh, pairs[i + 1], i == 0)
             if a == 0 and i < 3:
                 event(time + 0.2, multiply, cor, w_in, acc_c, yh, pairs[i + 1], i == 0)
-    hop = 3.3
-    for k, times in enumerate(((5.8, 7.2, 9.2, 10.6), (12.0, 13.4, 14.8, 16.2))):
+    hop = 3.4
+    for k, times in enumerate(((5.8, 7.2, 9.7, 11.1), (12.2, 13.6, 15.0, 16.4))):
         for (i, r), time in zip(order, times):
             event(time, mate_arrives, k, i, r)
             event(time + hop, swap_arrives, k, i, r)
             event(time + hop + 0.1, side_arrives, k, i, r, 0)
-            event(time + 2 * hop + 0.2, side_arrives, k, i, r, 1)
-    for i, time in enumerate((18.0, 19.4)):
+            event(time + 2 * hop + 0.6, side_arrives, k, i, r, 1)
+    for i, time in enumerate((18.1, 19.5)):
         event(time, mate_arrives, 2, i, 0)
-    event(19.6, after_twin, 0)
-    for i in range(1, 4):
-        event(19.7, multiply, tok, w_in, acc_p, there, pairs[i], i == 1)
-    event(20.7, multiply, tok, w_in, acc_p, there, pairs[4], False)
+    event(22.0, after_twin, 0)
+    for i in range(1, 5):
+        event(22.1, multiply, tok, w_in, acc_p, there, pairs[i], i == 1)
+    event(23.9, activate)
     for i in range(2):
-        event(20.8, swap_arrives, 2, i, 0)
-        event(20.8, side_arrives, 2, i, 0, 0)
-    event(20.9, activate)
+        event(24.0, swap_arrives, 2, i, 0)
+        event(24.0, side_arrives, 2, i, 0, 0)
     for _, _, what, args in sorted(events, key=lambda x: x[:2]):
         what(*args)
 
@@ -569,7 +571,7 @@
     read_rows()
     for a in range(2):
         whole(outs[a].at[:, pl.ds(0, 3 * cut)], (7, a), (7, a)).wait_recv()
-    for copy in loads[7:]:
+    for copy in loads[9:]:
         copy.wait()
     covers = [((0, 0), acc_p.at[pl.ds(0, 31 * n_tok // 32)])]
     covers += [((0, 1), acc_d.at[pl.ds(0, 31 * n_tok // 32)])]
@@ -650,6 +652,7 @@
             pltpu.VMEM((2, 4, 2, 2, shard, cut), BF16),
             pltpu.VMEM((2, 4, 2, 2, shard, cut), BF16),
             pltpu.VMEM((2, 4, shard, cut), BF16),
+            pltpu.VMEM((2, shard, local_ff), BF16),
             pltpu.VMEM((npass, 128), jnp.int32),
             pltpu.VMEM((npass, 128), jnp.int32),
             pltpu.VMEM((2, 2 * NT, npass, feat), F32),
@@ -660,7 +663,7 @@
             pltpu.VMEM((4 * NZ, 1, feat), F32),
             pltpu.SMEM((npass,), jnp.int32),
             pltpu.SMEM((npass,), jnp.int32),
-            pltpu.SemaphoreType.DMA((9,)),
+            pltpu.SemaphoreType.DMA((11,)),
             pltpu.SemaphoreType.DMA((13,)),
             pltpu.SemaphoreType.DMA((n_sem,)),
         ],

time: 71.2 us -> 71.1 us (level)
  no operation moved by 1% of the time
where the time goes in v6:
time: 71.1 us; the launch traced here: 71 us
  Pallas kernels  70.4 us (99%)
    pallas_call x1, Pallas kernels, fused(): pl.pallas_call(functools.partial(kernel, n_corpus // npass, scale_in, sca...  68.7 us
    pallas_call x1, Pallas kernels, handed_over(): pl.pallas_call(pass_through, out_shape=tuple((jax.ShapeDtypeStruct(x.shap...  1.68 us

profile of v6, /device:TPU:1, one launch (start us, length us, event | category | flops | bytes accessed | tf_op | source)
XLA Modules:
  0.0 71.0 jit_solution(4867235392107574188)
XLA Ops:
  0.6 68.7 %shard_map.94 = (bf16[64,1024]{1,0:T(8,128)(2,1)}, bf16[64,1024]{1,0:T(8,128)(2,1)}, bf16[16,256]{1,0:T(8,128)(2,1)}) custom-call(bf16[8,2,32,2048]{3,2,1,0:T(8,128)(2,1)} %bitcast.3, bf16[8,2,32,2048]{3,2,1,0:T(8,128)(2,1)} %bitcast.4, bf16[8,2,16,2048]{3,2,1,0:T(8,128)(2,1)} %bitcast.5, s32[8]{0:T(128)} %len_hbm.1, s32[8]{0:T(128)} %owner_hbm.1, ...), custom_call_target="tpu_custom_call" | custom-call | tf_op jit(solution)/shard_map/pallas_call | solution.py:630
  69.4 1.7 %shard_map.95 = (bf16[64,1024]{1,0:T(8,128)(2,1)}, bf16[64,1024]{1,0:T(8,128)(2,1)}, bf16[16,256]{1,0:T(8,128)(2,1)}) custom-call(bf16[64,1024]{1,0:T(8,128)(2,1)} %get-tuple-element.6.refs_0_, bf16[64,1024]{1,0:T(8,128)(2,1)} %get-tuple-element.7.refs_1_, bf16[16,256]{1,0:T(8,128)(2,1)} %get-tuple-element.8.refs_2_), custom_call_target="tpu_custom_call" | custom-call | tf_op jit(solution)/shard_map/pallas_call | solution.py:608

commit v7 on v6

--- a/solution.py
+++ b/solution.py
@@ -53,6 +53,7 @@
     r_out,
     fin,
     held,
+    index_rows,
     lens_here,
     lens_there,
     pool,
@@ -509,7 +510,8 @@
             out = jnp.zeros(shape, F32)
             for d in range(2 * NZ):
                 out = jnp.where(row == d, jnp.broadcast_to(letter_in[gg * 2 * NZ + d], shape), out)
-            index_ref[:, gg * feat : (gg + 1) * feat] = out.astype(BF16)
+            index_rows[:, gg * feat : (gg + 1) * feat] = out.astype(BF16)
+        load(index_rows, index_ref)
 
     outs = (new_in_ref, new_out_ref)
     sums = ((g_in, r_in, w_in), (g_out, r_out, w_out))
@@ -626,7 +628,6 @@
     feat = width // (2 * NT)
     rows_t, rows_c = n_tok // 16, n_corpus // 16
     any_spec = pl.BlockSpec(memory_space=pl.ANY)
-    vmem_spec = pl.BlockSpec(memory_space=pltpu.VMEM)
     return pl.pallas_call(
         functools.partial(kernel, n_corpus // npass, scale_in, scale_out),
         out_shape=(
@@ -635,7 +636,7 @@
             jax.ShapeDtypeStruct((2 * NZ, 2 * feat), BF16),
         ),
         in_specs=[any_spec] * 7,
-        out_specs=(any_spec, any_spec, vmem_spec),
+        out_specs=(any_spec, any_spec, any_spec),
         scratch_shapes=[
             pltpu.VMEM((16, 2, rows_t, width), BF16),
             pltpu.VMEM((16, 2, rows_t, width), BF16),
@@ -653,6 +654,7 @@
             pltpu.VMEM((2, 4, 2, 2, shard, cut), BF16),
             pltpu.VMEM((2, 4, shard, cut), BF16),
             pltpu.VMEM((2, shard, local_ff), BF16),
+            pltpu.VMEM((2 * NZ, 2 * feat), BF16),
             pltpu.VMEM((npass, 128), jnp.int32),
             pltpu.VMEM((npass, 128), jnp.int32),
             pltpu.VMEM((2, 2 * NT, npass, feat), F32),
@@ -663,7 +665,7 @@
             pltpu.VMEM((4 * NZ, 1, feat), F32),
             pltpu.SMEM((npass,), jnp.int32),
             pltpu.SMEM((npass,), jnp.int32),
-            pltpu.SemaphoreType.DMA((11,)),
+            pltpu.SemaphoreType.DMA((12,)),
             pltpu.SemaphoreType.DMA((13,)),
             pltpu.SemaphoreType.DMA((n_sem,)),
         ],

time: 71.1 us -> 70.5 us (level)
  no operation moved by 1% of the time
where the time goes in v7:
time: 70.5 us; the launch traced here: 70.4 us
  Pallas kernels  69.8 us (99%)
    pallas_call x1, Pallas kernels, fused(): pl.pallas_call(functools.partial(kernel, n_corpus // npass, scale_in, sca...  68.1 us
    pallas_call x1, Pallas kernels, handed_over(): pl.pallas_call(pass_through, out_shape=tuple((jax.ShapeDtypeStruct(x.shap...  1.68 us

profile of v7, /device:TPU:1, one launch (start us, length us, event | category | flops | bytes accessed | tf_op | source)
XLA Modules:
  0.0 70.4 jit_solution(12198728895086997088)
XLA Ops:
  0.6 68.1 %shard_map.94 = (bf16[64,1024]{1,0:T(8,128)(2,1)}, bf16[64,1024]{1,0:T(8,128)(2,1)}, bf16[16,256]{1,0:T(8,128)(2,1)}) custom-call(bf16[8,2,32,2048]{3,2,1,0:T(8,128)(2,1)} %bitcast.3, bf16[8,2,32,2048]{3,2,1,0:T(8,128)(2,1)} %bitcast.4, bf16[8,2,16,2048]{3,2,1,0:T(8,128)(2,1)} %bitcast.5, s32[8]{0:T(128)} %len_hbm.1, s32[8]{0:T(128)} %owner_hbm.1, ...), custom_call_target="tpu_custom_call" | custom-call | tf_op jit(solution)/shard_map/pallas_call | solution.py:631
  68.8 1.7 %shard_map.95 = (bf16[64,1024]{1,0:T(8,128)(2,1)}, bf16[64,1024]{1,0:T(8,128)(2,1)}, bf16[16,256]{1,0:T(8,128)(2,1)}) custom-call(bf16[64,1024]{1,0:T(8,128)(2,1)} %get-tuple-element.6.refs_0_, bf16[64,1024]{1,0:T(8,128)(2,1)} %get-tuple-element.7.refs_1_, bf16[16,256]{1,0:T(8,128)(2,1)} %get-tuple-element.8.refs_2_), custom_call_target="tpu_custom_call" | custom-call | tf_op jit(solution)/shard_map/pallas_call | solution.py:610

commit v8 on v7

--- a/solution.py
+++ b/solution.py
@@ -372,8 +372,8 @@
         event(22.1, multiply, tok, w_in, acc_p, there, pairs[i], i == 1)
     event(23.9, activate)
     for i in range(2):
-        event(24.0, swap_arrives, 2, i, 0)
-        event(24.0, side_arrives, 2, i, 0, 0)
+        event(22.2, swap_arrives, 2, i, 0)
+        event(22.2, side_arrives, 2, i, 0, 0)
     for _, _, what, args in sorted(events, key=lambda x: x[:2]):
         what(*args)
 

time: 70.5 us -> 71.1 us (level)
  no operation moved by 1% of the time
where the time goes in v8:
time: 71.1 us; the launch traced here: 71 us
  Pallas kernels  70.4 us (99%)
    pallas_call x1, Pallas kernels, fused(): pl.pallas_call(functools.partial(kernel, n_corpus // npass, scale_in, sca...  68.7 us
    pallas_call x1, Pallas kernels, handed_over(): pl.pallas_call(pass_through, out_shape=tuple((jax.ShapeDtypeStruct(x.shap...  1.68 us

profile of v8, /device:TPU:1, one launch (start us, length us, event | category | flops | bytes accessed | tf_op | source)
XLA Modules:
  0.0 71.0 jit_solution(408724702031890758)
XLA Ops:
  0.6 68.7 %shard_map.94 = (bf16[64,1024]{1,0:T(8,128)(2,1)}, bf16[64,1024]{1,0:T(8,128)(2,1)}, bf16[16,256]{1,0:T(8,128)(2,1)}) custom-call(bf16[8,2,32,2048]{3,2,1,0:T(8,128)(2,1)} %bitcast.3, bf16[8,2,32,2048]{3,2,1,0:T(8,128)(2,1)} %bitcast.4, bf16[8,2,16,2048]{3,2,1,0:T(8,128)(2,1)} %bitcast.5, s32[8]{0:T(128)} %len_hbm.1, s32[8]{0:T(128)} %owner_hbm.1, ...), custom_call_target="tpu_custom_call" | custom-call | tf_op jit(solution)/shard_map/pallas_call | solution.py:631
  69.3 1.7 %shard_map.95 = (bf16[64,1024]{1,0:T(8,128)(2,1)}, bf16[64,1024]{1,0:T(8,128)(2,1)}, bf16[16,256]{1,0:T(8,128)(2,1)}) custom-call(bf16[64,1024]{1,0:T(8,128)(2,1)} %get-tuple-element.6.refs_0_, bf16[64,1024]{1,0:T(8,128)(2,1)} %get-tuple-element.7.refs_1_, bf16[16,256]{1,0:T(8,128)(2,1)} %get-tuple-element.8.refs_2_), custom_call_target="tpu_custom_call" | custom-call | tf_op jit(solution)/shard_map/pallas_call | solution.py:610
